TPU v7x, 32 devices: a whole 2x2x4 slice. The times are simulated.
32 devices in a mesh: mom: 4 (over y, core), tr: 2 (over x), tc: 4 (over z).
Axes of the slice: x: 2, y: 2, z: 4, core: 2. Of those that a mesh axis runs over, the one named last changes fastest.
Arguments:
- start_rows: float32 [256, 8, 8192], P('tr', 'mom', 'tc'), may hold values from -6 to 6
- sigma_start: float32 [256, 8, 8192], P('tr', 'mom', 'tc'), may hold values from -6 to 6
- history: float32 [8, 8192, 8192], P('mom', 'tr', 'tc'), may hold values from -0.0625 to 0.0625
- interaction: float32 [2, 256, 8, 8192], P(None, 'tr', None, 'tc'), may hold values from -1.2 to 1.2
Outputs:
- first_rows: float32 [256, 8, 8192], P('tr', 'mom', 'tc')
- last_rows: float32 [256, 8, 8192], P('tr', 'mom', 'tc')
- last_sigma: float32 [256, 8, 8192], P('tr', 'mom', 'tc')
All inputs are finite; a program needn't handle non-finite values.
Results may differ from a plain program's by a relative error of at most 0.00011.
Values sent between devices are 32-bit elements; how exact they have to be, the bound alone decides.
A program may use at most 192 MiB of HBM per device.

v0:
```python
import jax
import jax.numpy as jnp
from jax import lax
from jax.sharding import PartitionSpec as P

CORRECTORS = 2


def relayout(energy):
    widened = lax.all_gather(energy, "tc", axis=2, tiled=True)
    return lax.all_to_all(widened, "tr", split_axis=2, concat_axis=0, tiled=True)


def body(start_rows, sigma_start, history, interaction):
    groups = lax.axis_size("mom")
    local_count = start_rows.shape[1]
    total_count = local_count * groups
    group_index = lax.axis_index("mom")
    momenta = group_index * local_count + jnp.arange(local_count, dtype=jnp.int32)
    shifts = jnp.arange(total_count, dtype=jnp.int32)
    green = start_rows
    energy = sigma_start
    spread_energy = relayout(energy)
    block_total = interaction.shape[0]
    results = []
    for block_index in range(block_total):
        weights_now = interaction[block_index]
        base_rows = green
        for sweep_index in range(CORRECTORS):
            energy_piece = spread_energy
            green = base_rows + lax.psum_scatter(
                jnp.einsum(
                    "rmt,mtc->rmc",
                    energy_piece,
                    history,
                    precision=lax.Precision.HIGHEST,
                    preferred_element_type=jnp.float32,
                ),
                "tr",
                scatter_dimension=0,
                tiled=True,
            )
            every_green = lax.all_gather(green, "mom", axis=1, tiled=True)
            wanted = jnp.mod(momenta[:, None] - shifts[None, :], total_count)
            select_table = (wanted[:, :, None] == shifts[None, None, :]).astype(jnp.float32)
            energy = jnp.einsum(
                "rdc,mdq,rqc->rmc",
                weights_now,
                select_table,
                every_green,
                precision=lax.Precision.HIGHEST,
            )
            if not (block_index == block_total - 1 and sweep_index == CORRECTORS - 1):
                spread_energy = relayout(energy)
        results.append(green)
    return (results[0], results[block_total - 1], energy)


def solution(mesh):
    return jax.shard_map(
        body,
        mesh=mesh,
        in_specs=(
            P("tr", "mom", "tc"),
            P("tr", "mom", "tc"),
            P("mom", "tr", "tc"),
            P(None, "tr", None, "tc"),
        ),
        out_specs=(P("tr", "mom", "tc"), P("tr", "mom", "tc"), P("tr", "mom", "tc")),
        check_vma=False,
    )
```

profile of v0, /device:TPU:0, one launch (start us, length us, event | category | flops | bytes accessed | tf_op | source)
XLA Modules:
  0.0 1946.4 jit_solution(9221414055732677260)
XLA Ops:
  7.2 5.1 copy.40
  12.4 152.4 %all-gather.9.cloned.1.call-done = f32[128,2,8192]{0,1,2:T(2,128)} async-done(((f32[128,2,2048]{0,1,2:T(2,128)}), f32[128,2,8192]{0,1,2:T(2,128)}) %all-gather.9.cloned.1.call-update) | async-done | bytes 8388624 | tf_op jit(solution)/shard_map/all_gather | solution.py:10
  164.9 97.4 %all_to_all.72 = f32[128,2,8192]{0,1,2:T(2,128)S(1)} all-to-all(f32[128,2,8192]{0,1,2:T(2,128)} %all-gather.9.cloned.1.call-done), channel_id=1, replica_groups=mesh['mom'=4,'tr'=2,'tc'=4] {'tr'}, dimensions={2} | all-to-all | bytes 16777216 | tf_op jit(solution)/shard_map/all_to_all | solution.py:11
  262.3 3.8 copy.41
  266.0 9.1 copy.42
  275.1 110.9 %convolution_bitcast_fusion.3 = f32[256,2,2048]{0,2,1:T(8,128)} fusion(f32[2,4096,2048]{2,1,0:T(8,128)} %param.6, f32[256,2,4096]{2,0,1:T(8,128)} %bitcast.75), kind=kOutput, calls=%fused_computation.13 | convolution fusion | flops 51539607552 | bytes 79691776 | tf_op jit(solution)/shard_map/rmt,mtc->rmc/dot_general | solution.py:32
  386.1 2.4 copy.44
  388.5 49.3 %reduce-scatter.5.cloned.1.call-done = f32[128,2,2048]{0,2,1:T(8,128)} async-done(((f32[256,2,2048]{0,2,1:T(8,128)}), f32[128,2,2048]{0,2,1:T(8,128)}) %reduce-scatter.5.cloned.1.call-update) | async-done | bytes 2097168 | tf_op jit(solution)/shard_map/reduce_scatter | solution.py:31
  437.8 3.7 add.49
  441.5 2.9 copy.45
  444.6 58.3 %all-gather.11.cloned.1.call-done = f32[128,8,2048]{2,0,1:T(8,128)} async-done(((f32[128,2,2048]{2,0,1:T(8,128)}), f32[128,8,2048]{2,0,1:T(8,128)}) %all-gather.11.cloned.1.call-update) | async-done | bytes 8388624 | tf_op jit(solution)/shard_map/all_gather | solution.py:43
  502.9 11.5 copy.89
  514.4 19.0 multiply_reduce_fusion.3
  533.4 4.1 copy.64
  537.6 149.7 %all-gather.13.cloned.1.call-done = f32[128,2,8192]{0,1,2:T(2,128)} async-done(((f32[128,2,2048]{0,1,2:T(2,128)}), f32[128,2,8192]{0,1,2:T(2,128)}) %all-gather.13.cloned.1.call-update) | async-done | bytes 8388624 | tf_op jit(solution)/shard_map/all_gather | solution.py:10
  687.3 97.8 %all_to_all.73 = f32[128,2,8192]{0,1,2:T(2,128)S(1)} all-to-all(f32[128,2,8192]{0,1,2:T(2,128)} %all-gather.13.cloned.1.call-done), channel_id=1, replica_groups=mesh['mom'=4,'tr'=2,'tc'=4] {'tr'}, dimensions={2} | all-to-all | bytes 16777216 | tf_op jit(solution)/shard_map/all_to_all | solution.py:11
  785.1 3.8 copy.46
  788.9 9.0 copy.47
  797.9 65.1 %convolution_bitcast_fusion.2 = f32[256,2,2048]{2,0,1:T(8,128)} fusion(f32[256,2,4096]{2,0,1:T(8,128)} %bitcast.72, f32[2,4096,2048]{2,1,0:T(8,128)} %param.6), kind=kOutput, calls=%fused_computation.12 | convolution fusion | flops 51539607552 | bytes 79691776 | tf_op jit(solution)/shard_map/rmt,mtc->rmc/dot_general | solution.py:32
  863.0 51.7 %reduce-scatter.7.cloned.1.call-done = f32[128,2,2048]{2,0,1:T(8,128)} async-done(((f32[256,2,2048]{2,0,1:T(8,128)}), f32[128,2,2048]{2,0,1:T(8,128)}) %reduce-scatter.7.cloned.1.call-update) | async-done | bytes 2097168 | tf_op jit(solution)/shard_map/reduce_scatter | solution.py:31
  914.8 4.2 copy_add_fusion
  919.2 58.2 %all-gather.15.cloned.1.call-done = f32[128,8,2048]{2,0,1:T(8,128)} async-done(((f32[128,2,2048]{2,0,1:T(8,128)}), f32[128,8,2048]{2,0,1:T(8,128)}) %all-gather.15.cloned.1.call-update) | async-done | bytes 8388624 | tf_op jit(solution)/shard_map/all_gather | solution.py:43
  977.4 8.2 copy.90
  985.6 9.1 multiply_reduce_fusion.2
  997.1 149.7 %all-gather.17.cloned.1.call-done = f32[128,2,8192]{0,1,2:T(2,128)} async-done(((f32[128,2,2048]{0,1,2:T(2,128)}), f32[128,2,8192]{0,1,2:T(2,128)}) %all-gather.17.cloned.1.call-update) | async-done | bytes 8388624 | tf_op jit(solution)/shard_map/all_gather | solution.py:10
  1146.8 97.6 %all_to_all.74 = f32[128,2,8192]{0,1,2:T(2,128)S(1)} all-to-all(f32[128,2,8192]{0,1,2:T(2,128)} %all-gather.17.cloned.1.call-done), channel_id=1, replica_groups=mesh['mom'=4,'tr'=2,'tc'=4] {'tr'}, dimensions={2} | all-to-all | bytes 16777216 | tf_op jit(solution)/shard_map/all_to_all | solution.py:11
  1244.4 3.8 copy.49
  1248.2 9.1 copy.50
  1257.3 65.2 %convolution_bitcast_fusion.1 = f32[256,2,2048]{2,0,1:T(8,128)} fusion(f32[256,2,4096]{2,0,1:T(8,128)} %bitcast.73, f32[2,4096,2048]{2,1,0:T(8,128)} %param.6), kind=kOutput, calls=%fused_computation.11 | convolution fusion | flops 51539607552 | bytes 79691776 | tf_op jit(solution)/shard_map/rmt,mtc->rmc/dot_general | solution.py:32
  1322.6 51.7 %reduce-scatter.9.cloned.1.call-done = f32[128,2,2048]{2,0,1:T(8,128)} async-done(((f32[256,2,2048]{2,0,1:T(8,128)}), f32[128,2,2048]{2,0,1:T(8,128)}) %reduce-scatter.9.cloned.1.call-update) | async-done | bytes 2097168 | tf_op jit(solution)/shard_map/reduce_scatter | solution.py:31
  1374.3 3.2 add.51
  1377.8 58.1 %all-gather.19.cloned.1.call-done = f32[128,8,2048]{2,0,1:T(8,128)} async-done(((f32[128,2,2048]{2,0,1:T(8,128)}), f32[128,8,2048]{2,0,1:T(8,128)}) %all-gather.19.cloned.1.call-update) | async-done | bytes 8388624 | tf_op jit(solution)/shard_map/all_gather | solution.py:43
  1435.9 11.5 copy.91
  1447.4 19.0 multiply_reduce_fusion.1
  1466.4 4.1 copy.80
  1470.6 149.7 %all-gather.21.cloned.1.call-done = f32[128,2,8192]{0,1,2:T(2,128)} async-done(((f32[128,2,2048]{0,1,2:T(2,128)}), f32[128,2,8192]{0,1,2:T(2,128)}) %all-gather.21.cloned.1.call-update) | async-done | bytes 8388624 | tf_op jit(solution)/shard_map/all_gather | solution.py:10
  1620.3 107.1 %all_to_all.75 = f32[128,2,8192]{0,1,2:T(2,128)S(1)} all-to-all(f32[128,2,8192]{0,1,2:T(2,128)} %all-gather.21.cloned.1.call-done), channel_id=1, replica_groups=mesh['mom'=4,'tr'=2,'tc'=4] {'tr'}, dimensions={2} | all-to-all | bytes 16777216 | tf_op jit(solution)/shard_map/all_to_all | solution.py:11
  1727.4 3.8 copy.51
  1731.2 9.0 copy.52
  1740.2 65.1 %convolution_bitcast_fusion = f32[256,2,2048]{2,0,1:T(8,128)} fusion(f32[256,2,4096]{2,0,1:T(8,128)} %bitcast.74, f32[2,4096,2048]{2,1,0:T(8,128)} %param.6), kind=kOutput, calls=%fused_computation.10 | convolution fusion | flops 51539607552 | bytes 79691776 | tf_op jit(solution)/shard_map/rmt,mtc->rmc/dot_general | solution.py:32
  1805.4 51.7 %reduce-scatter.11.cloned.1.call-done = f32[128,2,2048]{2,0,1:T(8,128)} async-done(((f32[256,2,2048]{2,0,1:T(8,128)}), f32[128,2,2048]{2,0,1:T(8,128)}) %reduce-scatter.11.cloned.1.call-update) | async-done | bytes 2097168 | tf_op jit(solution)/shard_map/reduce_scatter | solution.py:31
  1857.1 3.2 add.52
  1860.3 2.9 copy.53
  1863.2 4.5 copy.54
  1867.8 51.0 %all-gather.23.cloned.1.call-done = f32[128,8,2048]{2,0,1:T(8,128)} async-done(((f32[128,2,2048]{2,0,1:T(8,128)}), f32[128,8,2048]{2,0,1:T(8,128)}) %all-gather.23.cloned.1.call-update) | async-done | bytes 8388624 | tf_op jit(solution)/shard_map/all_gather | solution.py:43
  1918.7 8.2 copy.92
  1926.9 9.4 multiply_reduce_fusion
  1936.4 2.9 copy.99
  (31 shorter events, 3.6 us)
Async XLA Ops:
  7.2 157.7 %all-gather.9.cloned.1.call-start = ((), (), s32[]{:S(2)}) async-start(), calls=%async_computation.8 | async-start | bytes 10485760 | tf_op jit(solution)/shard_map/all_gather | solution.py:10
  12.4 425.4 %reduce-scatter.5.cloned.1.call-start = ((), (), s32[]{:S(2)}) async-start(), calls=%async_computation.9 | async-start | bytes 6291456 | tf_op jit(solution)/shard_map/reduce_scatter | solution.py:31
  275.1 111.0 %copy-start.1 = (f32[128,2,2048]{2,1,0:T(2,128)S(1)}, f32[128,2,2048]{2,1,0:T(2,128)}, u32[]{:S(2)}) copy-start(f32[128,2,2048]{2,1,0:T(2,128)} %param.4) | copy-start | bytes 6291460
  386.0 116.9 %all-gather.11.cloned.1.call-start = ((), (), s32[]{:S(2)}) async-start(), calls=%async_computation.10 | async-start | bytes 10485760 | tf_op jit(solution)/shard_map/all_gather | solution.py:43
  444.4 242.8 %all-gather.13.cloned.1.call-start = ((), (), s32[]{:S(2)}) async-start(), calls=%async_computation.11 | async-start | bytes 10485760 | tf_op jit(solution)/shard_map/all_gather | solution.py:10
  537.5 377.2 %reduce-scatter.7.cloned.1.call-start = ((), (), s32[]{:S(2)}) async-start(), calls=%async_computation.12 | async-start | bytes 6291456 | tf_op jit(solution)/shard_map/reduce_scatter | solution.py:31
  863.0 114.4 %all-gather.15.cloned.1.call-start = ((), (), s32[]{:S(2)}) async-start(), calls=%async_computation.13 | async-start | bytes 10485760 | tf_op jit(solution)/shard_map/all_gather | solution.py:43
  918.9 227.9 %all-gather.17.cloned.1.call-start = ((), (), s32[]{:S(2)}) async-start(), calls=%async_computation.14 | async-start | bytes 10485760 | tf_op jit(solution)/shard_map/all_gather | solution.py:10
  997.1 377.2 %reduce-scatter.9.cloned.1.call-start = ((), (), s32[]{:S(2)}) async-start(), calls=%async_computation.15 | async-start | bytes 6291456 | tf_op jit(solution)/shard_map/reduce_scatter | solution.py:31
  1257.3 117.0 %copy-start = (f32[128,2,2048]{2,0,1:T(8,128)S(1)}, f32[128,2,2048]{2,0,1:T(8,128)}, u32[]{:S(2)}) copy-start(f32[128,2,2048]{2,0,1:T(8,128)} %copy_add_fusion) | copy-start | bytes 6291460
  1322.5 113.4 %all-gather.19.cloned.1.call-start = ((), (), s32[]{:S(2)}) async-start(), calls=%async_computation.16 | async-start | bytes 10485760 | tf_op jit(solution)/shard_map/all_gather | solution.py:43
  1377.5 242.8 %all-gather.21.cloned.1.call-start = ((), (), s32[]{:S(2)}) async-start(), calls=%async_computation.17 | async-start | bytes 10485760 | tf_op jit(solution)/shard_map/all_gather | solution.py:10
  1470.6 386.6 %reduce-scatter.11.cloned.1.call-start = ((), (), s32[]{:S(2)}) async-start(), calls=%async_computation.18 | async-start | bytes 6291456 | tf_op jit(solution)/shard_map/reduce_scatter | solution.py:31
  1805.3 113.4 %all-gather.23.cloned.1.call-start = ((), (), s32[]{:S(2)}) async-start(), calls=%async_computation.19 | async-start | bytes 10485760 | tf_op jit(solution)/shard_map/all_gather | solution.py:43
Sparse Core Ops, SparseCore 0:
  12.5 152.3 all-gather.8
  386.1 51.5 reduce-scatter.4
  444.6 58.2 all-gather.10
  537.6 149.5 all-gather.12
  863.1 51.5 reduce-scatter.6
  919.1 58.2 all-gather.14
  997.2 149.5 all-gather.16
  1322.7 51.5 reduce-scatter.8
  1377.6 58.2 all-gather.18
  1470.7 149.5 all-gather.20
  1805.5 51.5 reduce-scatter.10
  1860.4 58.2 all-gather.22
where the time goes:
time: 1950 us
  waiting for transfers between devices  1030 us (53%)
  blocking collectives  400 us (21%)
  matrix products  344 us (18%)
  local copies, waits for them, and re-layouts  122 us (6%)
  other arithmetic  32.9 us (2%)
    all_gather x4, waiting for transfers between devices, relayout(): widened = lax.all_gather(energy, 'tc', axis=2, tiled=True)  602 us
    all_to_all x4, blocking collectives, relayout(): lax.all_to_all(widened, 'tr', split_axis=2, concat_axis=0, tiled=True)  400 us
    dot_general x4, matrix products, body(): jnp.einsum('rmt,mtc->rmc', energy_piece, history, precision=lax.Precision...  306 us
    all_gather x4, waiting for transfers between devices, body(): every_green = lax.all_gather(green, 'mom', axis=1, tiled=True)  226 us
    reduce_scatter x4, waiting for transfers between devices, body(): lax.psum_scatter(jnp.einsum('rmt,mtc->rmc', energy_piece, history, precis...  204 us
    unnamed x12, local copies, waits for them, and re-layouts  54.4 us
    all_to_all x8, local copies, waits for them, and re-layouts, relayout(): lax.all_to_all(widened, 'tr', split_axis=2, concat_axis=0, tiled=True)  51.3 us
  transfers between devices with their start and end apart: 12, of which 12 were waited for; matrix products, arithmetic and copies ran while one was open for 1% of the time, Pallas kernels for 0%

commit v1 on v0

v1 whole, which is shorter than its diff:
```python
import functools

import jax
import jax.numpy as jnp
from jax import lax
from jax.experimental import pallas as pl
from jax.experimental.pallas import tpu as pltpu
from jax.sharding import PartitionSpec as P


CORRECTORS = 2
CHUNKS = 4


def halves(x):
    high = x.astype(jnp.bfloat16)
    low = (x - high.astype(jnp.float32)).astype(jnp.bfloat16)
    return high, low


def product_kernel(count, ties, *refs):
    rows_refs, history_ref, out_refs = refs[:count], refs[count], refs[count + 1 + ties:]
    step = pl.program_id(2)
    rows = rows_refs[0].shape[2]
    total = count * rows
    x = jnp.concatenate([ref[0, 0] for ref in rows_refs], axis=0)
    x_high, x_low = halves(x)
    h_high, h_low = halves(history_ref[0])
    both = jnp.dot(
        jnp.concatenate([x_high, x_low], axis=0), h_high, preferred_element_type=jnp.float32
    )
    value = both[:total] + both[total:] + jnp.dot(x_high, h_low, preferred_element_type=jnp.float32)

    @pl.when(step == 0)
    def _():
        for index, ref in enumerate(out_refs):
            ref[0] = value[index * rows:(index + 1) * rows]

    @pl.when(step != 0)
    def _():
        for index, ref in enumerate(out_refs):
            ref[0] += value[index * rows:(index + 1) * rows]


def tie_spec(array):
    zeros = (0,) * array.ndim
    return pl.BlockSpec((1,) * (array.ndim - 2) + (8, 128), lambda *_: zeros)


def product(parts, history, ties):
    count = len(parts)
    pieces, momenta, rows, times = parts[0].shape
    columns = history.shape[2]
    tile_t = min(times, 1024)
    tile_c = min(columns, 1024)
    inner = times // tile_t
    steps = pieces * inner
    part_spec = pl.BlockSpec(
        (1, 1, rows, tile_t), lambda m, c, t: (t // inner, m, 0, t % inner)
    )
    return pl.pallas_call(
        functools.partial(product_kernel, count, len(ties)),
        grid=(momenta, columns // tile_c, steps),
        in_specs=[part_spec] * count
        + [pl.BlockSpec((1, tile_t, tile_c), lambda m, c, t: (m, t, c))]
        + [tie_spec(tie) for tie in ties],
        out_specs=[pl.BlockSpec((1, rows, tile_c), lambda m, c, t: (m, 0, c))] * count,
        out_shape=[jax.ShapeDtypeStruct((momenta, rows, columns), jnp.float32)] * count,
        compiler_params=pltpu.CompilerParams(vmem_limit_bytes=48 * 1024 * 1024),
        cost_estimate=pl.CostEstimate(
            flops=6 * count * momenta * rows * pieces * times * columns,
            bytes_accessed=4 * history.size,
            transcendentals=0,
        ),
    )(*parts, history, *ties)


def convolve_kernel(masks, *refs):
    weights_ref, block_refs, out_ref = refs[0], refs[1:1 + len(masks)], refs[-1]
    own_group = lax.axis_index("mom")
    total_count = weights_ref.shape[0]
    local_count = out_ref.shape[0]
    for own in range(local_count):
        total = None
        for mask, ref in zip(masks, block_refs):
            other_group = own_group ^ mask
            for other in range(local_count):
                shift = (own_group - other_group) * local_count + own - other + total_count
                term = weights_ref[lax.rem(shift, total_count)] * ref[other]
                total = term if total is None else total + term
        out_ref[own] = total


def convolution(weights, masks, blocks, ties):
    momenta, rows, columns = blocks[0].shape
    total_count = weights.shape[0]
    tile = min(columns, 1024)
    spec = pl.BlockSpec((momenta, rows, tile), lambda c: (0, 0, c))
    return pl.pallas_call(
        functools.partial(convolve_kernel, masks),
        grid=(columns // tile,),
        in_specs=[pl.BlockSpec((total_count, rows, tile), lambda c: (0, 0, c))]
        + [spec] * len(blocks)
        + [tie_spec(tie) for tie in ties],
        out_specs=spec,
        out_shape=jax.ShapeDtypeStruct(blocks[0].shape, jnp.float32),
        compiler_params=pltpu.CompilerParams(vmem_limit_bytes=48 * 1024 * 1024),
        cost_estimate=pl.CostEstimate(
            flops=2 * total_count * blocks[0].size,
            bytes_accessed=4 * (weights.size + (len(blocks) + 1) * blocks[0].size),
            transcendentals=0,
        ),
    )(weights, *blocks, *ties)


def body(start_rows, sigma_start, history, interaction):
    groups = lax.axis_size("mom")
    splits = lax.axis_size("tr")
    widths = lax.axis_size("tc")
    own_split = lax.axis_index("tr")
    pieces = widths // splits
    block_total = interaction.shape[0]
    rows = start_rows.shape[0] // CHUNKS

    def ring(shift):
        return [(source, (source + shift) % splits) for source in range(splits)]

    def relayout(energy):
        every = lax.all_gather(energy, "tc", axis=0)
        sent = []
        for shift in range(1, splits):
            target = (own_split + shift) % splits
            sent.append(lax.dynamic_slice_in_dim(every, target * pieces, pieces, 0))
        parts = [lax.dynamic_slice_in_dim(every, own_split * pieces, pieces, 0)]
        for shift in range(1, splits):
            parts.append(lax.ppermute(sent[shift - 1], "tr", ring(shift)))
        return parts, sent

    def reduce_rows(partial):
        total = partial[0]
        for shift in range(1, splits):
            total = total + lax.ppermute(partial[shift], "tr", ring(-shift))
        return total

    masks = tuple(range(groups))

    def spread(green):
        blocks = [green]
        for mask in masks[1:]:
            swap = [(source, source ^ mask) for source in range(groups)]
            blocks.append(lax.ppermute(green, "mom", swap))
        return blocks

    def cut(array, chunk):
        return jnp.swapaxes(array[chunk * rows:(chunk + 1) * rows], 0, 1)

    weights = [
        [cut(interaction[block], chunk) for chunk in range(CHUNKS)] for block in range(block_total)
    ]
    energies = [None] * CHUNKS
    greens = [cut(start_rows, chunk) for chunk in range(CHUNKS)]
    bases = list(greens)
    spreads = [relayout(cut(sigma_start, chunk)) for chunk in range(CHUNKS)]
    results = [[None] * CHUNKS for _ in range(block_total)]
    steps = [
        (block, sweep, chunk)
        for block in range(block_total)
        for sweep in range(CORRECTORS)
        for chunk in range(CHUNKS)
    ]

    def finish(position, blocks, ties):
        step = steps[position]
        block, _, chunk = step
        energy = convolution(weights[block][chunk], masks, blocks, ties)
        if step[:2] == steps[-1][:2]:
            energies[chunk] = energy
        else:
            spreads[chunk] = relayout(energy)

    waiting = None
    for position, step in enumerate(steps):
        block, sweep, chunk = step
        ties = []
        if position + 1 < len(steps):
            ties += spreads[steps[position + 1][2]][1]
        if waiting is not None:
            ties.append(waiting[1][0])
        partial = product(spreads[chunk][0], history, ties)
        if waiting is not None:
            finish(*waiting, partial[:1])
        if sweep == 0:
            bases[chunk] = greens[chunk]
        green = bases[chunk] + reduce_rows(partial)
        greens[chunk] = green
        if sweep == CORRECTORS - 1:
            results[block][chunk] = green
        waiting = (position, spread(green))
    finish(*waiting, [])

    def join(chunks):
        return jnp.concatenate([jnp.swapaxes(chunk, 0, 1) for chunk in chunks], axis=0)

    return (join(results[0]), join(results[block_total - 1]), join(energies))


def solution(mesh):
    return jax.shard_map(
        body,
        mesh=mesh,
        in_specs=(
            P("tr", "mom", "tc"),
            P("tr", "mom", "tc"),
            P("mom", "tr", "tc"),
            P(None, "tr", None, "tc"),
        ),
        out_specs=(P("tr", "mom", "tc"), P("tr", "mom", "tc"), P("tr", "mom", "tc")),
        check_vma=False,
    )
```

time: 1950 us -> 1200 us (0.62)
  waiting for transfers between devices: 1030 us -> 473 us
  Pallas kernels: 0 us -> 494 us
  blocking collectives: 400 us -> 0 us
  matrix products: 344 us -> 0 us
  starting transfers between devices: 0.99 us -> 80.2 us
  other arithmetic: 32.9 us -> 11.9 us
    all_gather x8 -> x16, waiting for transfers between devices: 827 us -> 84.8 us  [relayout(): every = lax.all_gather(energy, 'tc', axis=0)]
    pallas_call x0 -> x32, Pallas kernels: none -> 494 us  [the longest x16 464 us: product(): pl.pallas_call(functools.partial(product_kernel, count, len(ties)), grid=...]
    all_to_all x4 -> x0, blocking collectives: 400 us -> none  [relayout(): lax.all_to_all(widened, 'tr', split_axis=2, concat_axis=0, tiled=True)]
    ppermute x0 -> x80, waiting for transfers between devices: none -> 388 us  [the longest x16 189 us: reduce_rows(): total = total + lax.ppermute(partial[shift], 'tr', ring(-shift))]
    dot_general x6 -> x0, matrix products: 344 us -> none  [the longest x4 306 us: body(): jnp.einsum('rmt,mtc->rmc', energy_piece, history, precision=lax.Precision...]
    reduce_scatter x4 -> x0, waiting for transfers between devices: 204 us -> none  [body(): lax.psum_scatter(jnp.einsum('rmt,mtc->rmc', energy_piece, history, precis...]
    ppermute x0 -> x80, starting transfers between devices: none -> 67.8 us  [the longest x48 31.9 us: spread(): blocks.append(lax.ppermute(green, 'mom', swap))]
    all_to_all x8 -> x0, local copies, waits for them, and re-layouts: 51.3 us -> none  [relayout(): lax.all_to_all(widened, 'tr', split_axis=2, concat_axis=0, tiled=True)]
  transfers between devices with their start and end apart: 12 -> 96, of which waited for: 12 -> 36; matrix products, arithmetic and copies ran while one was open for 1% -> 9% of each run, Pallas kernels for 0% -> 41%
where the time goes in v1:
time: 1200 us; the launch traced here: 1190 us
  Pallas kernels  494 us (41%)
  waiting for transfers between devices  473 us (39%)
  local copies, waits for them, and re-layouts  118 us (10%)
  starting transfers between devices  80.2 us (7%)
  between operations  15.2 us (1%)
    pallas_call x16, Pallas kernels, product(): pl.pallas_call(functools.partial(product_kernel, count, len(ties)), grid=...  464 us
    ppermute x16, waiting for transfers between devices, reduce_rows(): total = total + lax.ppermute(partial[shift], 'tr', ring(-shift))  189 us
    ppermute x16, waiting for transfers between devices, relayout(): parts.append(lax.ppermute(sent[shift - 1], 'tr', ring(shift)))  154 us
    all_gather x16, waiting for transfers between devices, relayout(): every = lax.all_gather(energy, 'tc', axis=0)  84.8 us
    unnamed x143, local copies, waits for them, and re-layouts  58.5 us
    ppermute x48, waiting for transfers between devices, spread(): blocks.append(lax.ppermute(green, 'mom', swap))  44.5 us
    ppermute x48, starting transfers between devices, spread(): blocks.append(lax.ppermute(green, 'mom', swap))  31.9 us
    pallas_call x16, Pallas kernels, convolution(): pl.pallas_call(functools.partial(convolve_kernel, masks), grid=(columns /...  29.8 us
  transfers between devices with their start and end apart: 96, of which 36 were waited for; matrix products, arithmetic and copies ran while one was open for 9% of the time, Pallas kernels for 41%

profile of v1, /device:TPU:0, one launch (start us, length us, event | category | flops | bytes accessed | tf_op | source)
XLA Modules:
  0.0 1192.0 jit_solution(11940506796787730600)
XLA Ops:
  13.7 44.9 %all-gather.33.cloned.1.call-done = f32[8,32,2048]{2,1,0:T(8,128)} async-done(((f32[2,32,2048]{2,1,0:T(8,128)}), f32[8,32,2048]{2,1,0:T(8,128)}) %all-gather.33.cloned.1.call-update) | async-done | bytes 2097168 | tf_op jit(solution)/shard_map/all_gather | solution.py:129
  62.8 12.6 %fusion = (f32[1,32,8,2048]{3,2,1,0:T(8,128)}, f32[1,32,8,2048]{3,2,1,0:T(8,128)}, f32[1,32,8,2048]{3,2,1,0:T(8,128)}, f32[1,32,8,2048]{3,2,1,0:T(8,128)}, f32[1...) fusion(f32[2,128,8,2048]{3,2,1,0:T(8,128)} %param.7), kind=kLoop, calls=%fused_computation.67 | loop fusion | bytes 33554432 | tf_op jit(solution)/shard_map/slice | solution.py:155
  75.4 29.2 %all-gather.35.cloned.1.call-done = f32[8,32,2048]{2,1,0:T(8,128)} async-done(((f32[2,32,2048]{2,1,0:T(8,128)}), f32[8,32,2048]{2,1,0:T(8,128)}) %all-gather.35.cloned.1.call-update) | async-done | bytes 2097168 | tf_op jit(solution)/shard_map/all_gather | solution.py:129
  109.2 29.2 %shard_map.67 = (f32[2,32,2048]{2,1,0:T(8,128)S(1)}, f32[2,32,2048]{2,1,0:T(8,128)S(1)}) custom-call(f32[2,2,32,2048]{3,2,1,0:T(8,128)S(1)} %get-tuple-element.118.refs_0_, f32[2,2,32,2048]{3,2,1,0:T(8,128)S(1)} %collective-permute-done.refs_1_, f32[2,4096,2048]{2,1,0:T(8,128)} %refs_2_.31, f32[2,2,32,2048]{3,2,1,0:T(8,128)} %get-tuple-element.116.refs_3_), custom_call_target="tpu_custom_call" | custom-call | flops 6442450944 | bytes 67108864 | tf_op jit(solution)/shard_map/pallas_call | solution.py:61
  141.5 9.2 all-gather.37.cloned.1.call-done
  157.3 29.3 %shard_map.68 = (f32[2,32,2048]{2,1,0:T(8,128)S(1)}, f32[2,32,2048]{2,1,0:T(8,128)S(1)}) custom-call(f32[2,2,32,2048]{3,2,1,0:T(8,128)S(1)} %copy-done.36, f32[2,2,32,2048]{3,2,1,0:T(8,128)} %collective-permute-done.5.refs_1_, f32[2,4096,2048]{2,1,0:T(8,128)} %refs_2_.31, f32[2,2,32,2048]{3,2,1,0:T(8,128)S(1)} %get-tuple-element.110.refs_3_, ...), custom_call_target="tpu_custom_call" | custom-call | flops 6442450944 | bytes 67108864 | tf_op jit(solution)/shard_map/pallas_call | solution.py:61
  199.4 26.5 %collective-permute-done.7 = f32[2,32,2048]{2,1,0:T(8,128)S(1)} collective-permute-done((f32[2,32,2048]{2,1,0:T(8,128)}, f32[2,32,2048]{2,1,0:T(8,128)S(1)}, u32[]{:S(2)}, u32[]{:S(2)}) %collective-permute-start.7) | collective-permute-done | bytes 524320 | tf_op jit(solution)/shard_map/ppermute | solution.py:142
  230.3 29.0 %shard_map.70 = (f32[2,32,2048]{2,1,0:T(8,128)S(1)}, f32[2,32,2048]{2,1,0:T(8,128)S(1)}) custom-call(f32[2,2,32,2048]{3,2,1,0:T(8,128)S(1)} %copy-done.14, f32[2,2,32,2048]{3,2,1,0:T(8,128)} %collective-permute-done.11.refs_1_, f32[2,4096,2048]{2,1,0:T(8,128)} %refs_2_.31, f32[2,2,32,2048]{3,2,1,0:T(8,128)S(1)} %get-tuple-element.119.refs_3_, ...), custom_call_target="tpu_custom_call" | custom-call | flops 6442450944 | bytes 67108864 | tf_op jit(solution)/shard_map/pallas_call | solution.py:61
  268.4 8.7 collective-permute-done.13
  282.3 16.2 %collective-permute-done.12.refs_1_ = f32[2,2,32,2048]{3,2,1,0:T(8,128)} collective-permute-done((f32[2,2,32,2048]{3,2,1,0:T(8,128)}, f32[2,2,32,2048]{3,2,1,0:T(8,128)}, u32[]{:S(2)}, u32[]{:S(2)}) %collective-permute-start.12) | collective-permute-done | bytes 1048608 | tf_op jit(solution)/shard_map/ppermute | solution.py:136
  298.4 29.0 %shard_map.72 = (f32[2,32,2048]{2,1,0:T(8,128)S(1)}, f32[2,32,2048]{2,1,0:T(8,128)S(1)}) custom-call(f32[2,2,32,2048]{3,2,1,0:T(8,128)S(1)} %copy-done.15, f32[2,2,32,2048]{3,2,1,0:T(8,128)} %collective-permute-done.12.refs_1_, f32[2,4096,2048]{2,1,0:T(8,128)} %refs_2_.31, f32[2,2,32,2048]{3,2,1,0:T(8,128)S(1)} %get-tuple-element.104.refs_3_, ...), custom_call_target="tpu_custom_call" | custom-call | flops 6442450944 | bytes 67108864 | tf_op jit(solution)/shard_map/pallas_call | solution.py:61
  339.8 26.3 %collective-permute-done.14 = f32[2,32,2048]{2,1,0:T(8,128)S(1)} collective-permute-done((f32[2,32,2048]{2,1,0:T(8,128)}, f32[2,32,2048]{2,1,0:T(8,128)S(1)}, u32[]{:S(2)}, u32[]{:S(2)}) %collective-permute-start.14) | collective-permute-done | bytes 524320 | tf_op jit(solution)/shard_map/ppermute | solution.py:142
  370.3 29.0 %shard_map.73 = (f32[2,32,2048]{2,1,0:T(8,128)S(1)}, f32[2,32,2048]{2,1,0:T(8,128)S(1)}) custom-call(f32[2,2,32,2048]{3,2,1,0:T(8,128)S(1)} %copy-done.20, f32[2,2,32,2048]{3,2,1,0:T(8,128)} %collective-permute-done.6.refs_1_, f32[2,4096,2048]{2,1,0:T(8,128)} %refs_2_.31, f32[2,2,32,2048]{3,2,1,0:T(8,128)S(1)} %get-tuple-element.100.refs_3_, ...), custom_call_target="tpu_custom_call" | custom-call | flops 6442450944 | bytes 67108864 | tf_op jit(solution)/shard_map/pallas_call | solution.py:61
  403.7 13.0 %collective-permute-done.15 = f32[2,32,2048]{2,1,0:T(8,128)S(1)} collective-permute-done((f32[2,32,2048]{2,1,0:T(8,128)}, f32[2,32,2048]{2,1,0:T(8,128)S(1)}, u32[]{:S(2)}, u32[]{:S(2)}) %collective-permute-start.15) | collective-permute-done | bytes 524320 | tf_op jit(solution)/shard_map/ppermute | solution.py:142
  422.9 15.8 %collective-permute-done.16.refs_1_ = f32[2,2,32,2048]{3,2,1,0:T(8,128)} collective-permute-done((f32[2,2,32,2048]{3,2,1,0:T(8,128)}, f32[2,2,32,2048]{3,2,1,0:T(8,128)}, u32[]{:S(2)}, u32[]{:S(2)}) %collective-permute-start.16) | collective-permute-done | bytes 1048608 | tf_op jit(solution)/shard_map/ppermute | solution.py:136
  438.7 28.8 %shard_map.75 = (f32[2,32,2048]{2,1,0:T(8,128)S(1)}, f32[2,32,2048]{2,1,0:T(8,128)S(1)}) custom-call(f32[2,2,32,2048]{3,2,1,0:T(8,128)S(1)} %copy-done.16, f32[2,2,32,2048]{3,2,1,0:T(8,128)} %collective-permute-done.16.refs_1_, f32[2,4096,2048]{2,1,0:T(8,128)} %refs_2_.31, f32[2,2,32,2048]{3,2,1,0:T(8,128)S(1)} %get-tuple-element.98.refs_3_, ...), custom_call_target="tpu_custom_call" | custom-call | flops 6442450944 | bytes 67108864 | tf_op jit(solution)/shard_map/pallas_call | solution.py:61
  472.9 13.0 %collective-permute-done.20 = f32[2,32,2048]{2,1,0:T(8,128)S(1)} collective-permute-done((f32[2,32,2048]{2,1,0:T(8,128)}, f32[2,32,2048]{2,1,0:T(8,128)S(1)}, u32[]{:S(2)}, u32[]{:S(2)}) %collective-permute-start.20) | collective-permute-done | bytes 524320 | tf_op jit(solution)/shard_map/ppermute | solution.py:142
  491.0 16.0 %collective-permute-done.21.refs_1_ = f32[2,2,32,2048]{3,2,1,0:T(8,128)} collective-permute-done((f32[2,2,32,2048]{3,2,1,0:T(8,128)}, f32[2,2,32,2048]{3,2,1,0:T(8,128)}, u32[]{:S(2)}, u32[]{:S(2)}) %collective-permute-start.21) | collective-permute-done | bytes 1048608 | tf_op jit(solution)/shard_map/ppermute | solution.py:136
  507.0 29.0 %shard_map.77 = (f32[2,32,2048]{2,1,0:T(8,128)S(1)}, f32[2,32,2048]{2,1,0:T(8,128)S(1)}) custom-call(f32[2,2,32,2048]{3,2,1,0:T(8,128)S(1)} %copy-done.25, f32[2,2,32,2048]{3,2,1,0:T(8,128)} %collective-permute-done.21.refs_1_, f32[2,4096,2048]{2,1,0:T(8,128)} %refs_2_.31, f32[2,2,32,2048]{3,2,1,0:T(8,128)S(1)} %get-tuple-element.101.refs_3_, ...), custom_call_target="tpu_custom_call" | custom-call | flops 6442450944 | bytes 67108864 | tf_op jit(solution)/shard_map/pallas_call | solution.py:61
  539.1 11.6 all-gather.53.cloned.1.call-start
  552.8 13.0 %collective-permute-done.25 = f32[2,32,2048]{2,1,0:T(8,128)S(1)} collective-permute-done((f32[2,32,2048]{2,1,0:T(8,128)}, f32[2,32,2048]{2,1,0:T(8,128)S(1)}, u32[]{:S(2)}, u32[]{:S(2)}) %collective-permute-start.25) | collective-permute-done | bytes 524320 | tf_op jit(solution)/shard_map/ppermute | solution.py:142
  571.8 14.2 %collective-permute-done.26.refs_1_ = f32[2,2,32,2048]{3,2,1,0:T(8,128)} collective-permute-done((f32[2,2,32,2048]{3,2,1,0:T(8,128)}, f32[2,2,32,2048]{3,2,1,0:T(8,128)}, u32[]{:S(2)}, u32[]{:S(2)}) %collective-permute-start.26) | collective-permute-done | bytes 1048608 | tf_op jit(solution)/shard_map/ppermute | solution.py:136
  586.0 28.9 %shard_map.79 = (f32[2,32,2048]{2,1,0:T(8,128)S(1)}, f32[2,32,2048]{2,1,0:T(8,128)S(1)}) custom-call(f32[2,2,32,2048]{3,2,1,0:T(8,128)S(1)} %get-tuple-element.102.refs_0_, f32[2,2,32,2048]{3,2,1,0:T(8,128)} %collective-permute-done.26.refs_1_, f32[2,4096,2048]{2,1,0:T(8,128)} %refs_2_.31, f32[2,2,32,2048]{3,2,1,0:T(8,128)S(1)} %get-tuple-element.96.refs_3_, ...), custom_call_target="tpu_custom_call" | custom-call | flops 6442450944 | bytes 67108864 | tf_op jit(solution)/shard_map/pallas_call | solution.py:61
  623.2 12.8 %collective-permute-done.30 = f32[2,32,2048]{2,1,0:T(8,128)S(1)} collective-permute-done((f32[2,32,2048]{2,1,0:T(8,128)S(1)}, f32[2,32,2048]{2,1,0:T(8,128)S(1)}, u32[]{:S(2)}, u32[]{:S(2)}) %collective-permute-start.30) | collective-permute-done | bytes 524320 | tf_op jit(solution)/shard_map/ppermute | solution.py:142
  642.7 12.7 %collective-permute-done.31.refs_1_ = f32[2,2,32,2048]{3,2,1,0:T(8,128)} collective-permute-done((f32[2,2,32,2048]{3,2,1,0:T(8,128)S(1)}, f32[2,2,32,2048]{3,2,1,0:T(8,128)}, u32[]{:S(2)}, u32[]{:S(2)}) %collective-permute-start.31) | collective-permute-done | bytes 1048608 | tf_op jit(solution)/shard_map/ppermute | solution.py:136
  655.4 29.1 %shard_map.81 = (f32[2,32,2048]{2,1,0:T(8,128)S(1)}, f32[2,32,2048]{2,1,0:T(8,128)S(1)}) custom-call(f32[2,2,32,2048]{3,2,1,0:T(8,128)S(1)} %copy-done.26, f32[2,2,32,2048]{3,2,1,0:T(8,128)} %collective-permute-done.31.refs_1_, f32[2,4096,2048]{2,1,0:T(8,128)} %refs_2_.31, f32[2,2,32,2048]{3,2,1,0:T(8,128)} %get-tuple-element.92.refs_3_, ...), custom_call_target="tpu_custom_call" | custom-call | flops 6442450944 | bytes 67108864 | tf_op jit(solution)/shard_map/pallas_call | solution.py:61
  706.8 13.6 %collective-permute-done.39.refs_1_ = f32[2,2,32,2048]{3,2,1,0:T(8,128)} collective-permute-done((f32[2,2,32,2048]{3,2,1,0:T(8,128)}, f32[2,2,32,2048]{3,2,1,0:T(8,128)}, u32[]{:S(2)}, u32[]{:S(2)}) %collective-permute-start.39) | collective-permute-done | bytes 1048608 | tf_op jit(solution)/shard_map/ppermute | solution.py:136
  720.4 29.0 %shard_map.83 = (f32[2,32,2048]{2,1,0:T(8,128)S(1)}, f32[2,32,2048]{2,1,0:T(8,128)S(1)}) custom-call(f32[2,2,32,2048]{3,2,1,0:T(8,128)S(1)} %copy-done.22, f32[2,2,32,2048]{3,2,1,0:T(8,128)} %collective-permute-done.39.refs_1_, f32[2,4096,2048]{2,1,0:T(8,128)} %refs_2_.31, f32[2,2,32,2048]{3,2,1,0:T(8,128)S(1)} %get-tuple-element.90.refs_3_, ...), custom_call_target="tpu_custom_call" | custom-call | flops 6442450944 | bytes 67108864 | tf_op jit(solution)/shard_map/pallas_call | solution.py:61
  759.0 8.8 collective-permute-done.44
  772.6 12.8 %collective-permute-done.48.refs_1_ = f32[2,2,32,2048]{3,2,1,0:T(8,128)} collective-permute-done((f32[2,2,32,2048]{3,2,1,0:T(8,128)}, f32[2,2,32,2048]{3,2,1,0:T(8,128)}, u32[]{:S(2)}, u32[]{:S(2)}) %collective-permute-start.48) | collective-permute-done | bytes 1048608 | tf_op jit(solution)/shard_map/ppermute | solution.py:136
  785.5 29.0 %shard_map.86 = (f32[2,32,2048]{2,1,0:T(8,128)S(1)}, f32[2,32,2048]{2,1,0:T(8,128)S(1)}) custom-call(f32[2,2,32,2048]{3,2,1,0:T(8,128)S(1)} %copy-done.23, f32[2,2,32,2048]{3,2,1,0:T(8,128)} %collective-permute-done.48.refs_1_, f32[2,4096,2048]{2,1,0:T(8,128)} %refs_2_.31, f32[2,2,32,2048]{3,2,1,0:T(8,128)S(1)} %get-tuple-element.93.refs_3_, ...), custom_call_target="tpu_custom_call" | custom-call | flops 6442450944 | bytes 67108864 | tf_op jit(solution)/shard_map/pallas_call | solution.py:61
  824.0 8.9 collective-permute-done.53
  837.8 12.0 %collective-permute-done.52.refs_1_ = f32[2,2,32,2048]{3,2,1,0:T(8,128)} collective-permute-done((f32[2,2,32,2048]{3,2,1,0:T(8,128)}, f32[2,2,32,2048]{3,2,1,0:T(8,128)}, u32[]{:S(2)}, u32[]{:S(2)}) %collective-permute-start.52) | collective-permute-done | bytes 1048608 | tf_op jit(solution)/shard_map/ppermute | solution.py:136
  849.7 29.0 %shard_map.88 = (f32[2,32,2048]{2,1,0:T(8,128)S(1)}, f32[2,32,2048]{2,1,0:T(8,128)S(1)}) custom-call(f32[2,2,32,2048]{3,2,1,0:T(8,128)S(1)} %copy-done.24, f32[2,2,32,2048]{3,2,1,0:T(8,128)} %collective-permute-done.52.refs_1_, f32[2,4096,2048]{2,1,0:T(8,128)} %refs_2_.31, f32[2,2,32,2048]{3,2,1,0:T(8,128)S(1)} %get-tuple-element.88.refs_3_, ...), custom_call_target="tpu_custom_call" | custom-call | flops 6442450944 | bytes 67108864 | tf_op jit(solution)/shard_map/pallas_call | solution.py:61
  888.2 8.9 collective-permute-done.54
  902.0 11.2 collective-permute-done.43.refs_1_
  913.2 29.2 %shard_map.89 = (f32[2,32,2048]{2,1,0:T(8,128)S(1)}, f32[2,32,2048]{2,1,0:T(8,128)S(1)}) custom-call(f32[2,2,32,2048]{3,2,1,0:T(8,128)S(1)} %copy-done.21, f32[2,2,32,2048]{3,2,1,0:T(8,128)} %collective-permute-done.43.refs_1_, f32[2,4096,2048]{2,1,0:T(8,128)} %refs_2_.31, f32[2,2,32,2048]{3,2,1,0:T(8,128)S(1)} %get-tuple-element.82.refs_3_, ...), custom_call_target="tpu_custom_call" | custom-call | flops 6442450944 | bytes 67108864 | tf_op jit(solution)/shard_map/pallas_call | solution.py:61
  947.7 13.0 %collective-permute-done.55 = f32[2,32,2048]{2,1,0:T(8,128)S(1)} collective-permute-done((f32[2,32,2048]{2,1,0:T(8,128)}, f32[2,32,2048]{2,1,0:T(8,128)S(1)}, u32[]{:S(2)}, u32[]{:S(2)}) %collective-permute-start.55) | collective-permute-done | bytes 524320 | tf_op jit(solution)/shard_map/ppermute | solution.py:142
  964.1 11.9 %collective-permute-done.56.refs_1_ = f32[2,2,32,2048]{3,2,1,0:T(8,128)} collective-permute-done((f32[2,2,32,2048]{3,2,1,0:T(8,128)}, f32[2,2,32,2048]{3,2,1,0:T(8,128)}, u32[]{:S(2)}, u32[]{:S(2)}) %collective-permute-start.56) | collective-permute-done | bytes 1048608 | tf_op jit(solution)/shard_map/ppermute | solution.py:136
  976.0 29.0 %shard_map.91 = (f32[2,32,2048]{2,1,0:T(8,128)S(1)}, f32[2,32,2048]{2,1,0:T(8,128)S(1)}) custom-call(f32[2,2,32,2048]{3,2,1,0:T(8,128)S(1)} %copy-done.35, f32[2,2,32,2048]{3,2,1,0:T(8,128)} %collective-permute-done.56.refs_1_, f32[2,4096,2048]{2,1,0:T(8,128)} %refs_2_.31, f32[2,2,32,2048]{3,2,1,0:T(8,128)} %get-tuple-element.83.refs_3_, ...), custom_call_target="tpu_custom_call" | custom-call | flops 6442450944 | bytes 67108864 | tf_op jit(solution)/shard_map/pallas_call | solution.py:61
  1007.0 12.8 %collective-permute-done.60 = f32[2,32,2048]{2,1,0:T(8,128)S(1)} collective-permute-done((f32[2,32,2048]{2,1,0:T(8,128)S(1)}, f32[2,32,2048]{2,1,0:T(8,128)S(1)}, u32[]{:S(2)}, u32[]{:S(2)}) %collective-permute-start.60) | collective-permute-done | bytes 524320 | tf_op jit(solution)/shard_map/ppermute | solution.py:142
  1024.3 18.1 %collective-permute-done.61.refs_1_ = f32[2,2,32,2048]{3,2,1,0:T(8,128)} collective-permute-done((f32[2,2,32,2048]{3,2,1,0:T(8,128)}, f32[2,2,32,2048]{3,2,1,0:T(8,128)}, u32[]{:S(2)}, u32[]{:S(2)}) %collective-permute-start.61) | collective-permute-done | bytes 1048608 | tf_op jit(solution)/shard_map/ppermute | solution.py:136
  1042.4 28.8 %shard_map.93 = (f32[2,32,2048]{2,1,0:T(8,128)S(1)}, f32[2,32,2048]{2,1,0:T(8,128)S(1)}) custom-call(f32[2,2,32,2048]{3,2,1,0:T(8,128)S(1)} %copy-done.38, f32[2,2,32,2048]{3,2,1,0:T(8,128)} %collective-permute-done.61.refs_1_, f32[2,4096,2048]{2,1,0:T(8,128)} %refs_2_.31, f32[2,2,32,2048]{3,2,1,0:T(8,128)S(1)} %get-tuple-element.85.refs_3_, ...), custom_call_target="tpu_custom_call" | custom-call | flops 6442450944 | bytes 67108864 | tf_op jit(solution)/shard_map/pallas_call | solution.py:61
  1080.6 28.6 %shard_map.94 = (f32[2,32,2048]{2,1,0:T(8,128)S(1)}, f32[2,32,2048]{2,1,0:T(8,128)S(1)}) custom-call(f32[2,2,32,2048]{3,2,1,0:T(8,128)S(1)} %get-tuple-element.86.refs_0_, f32[2,2,32,2048]{3,2,1,0:T(8,128)S(1)} %collective-permute-done.66.refs_1_, f32[2,4096,2048]{2,1,0:T(8,128)} %refs_2_.31, f32[2,32,2048]{2,1,0:T(8,128)S(1)} %add_add_fusion.1.refs_3_.refs_1_), custom_call_target="tpu_custom_call" | custom-call | flops 6442450944 | bytes 67108864 | tf_op jit(solution)/shard_map/pallas_call | solution.py:61
  1114.5 9.0 collective-permute-done.67
  1125.7 10.2 collective-permute-done.73.refs_4_
  1148.1 10.2 collective-permute-done.76.refs_4_
  1170.6 9.8 collective-permute-done.79.refs_4_
  (373 shorter events, 246.4 us)
Async XLA Ops:
  7.2 51.4 %all-gather.33.cloned.1.call-start = ((), (), s32[]{:S(2)}) async-start(), calls=%async_computation | async-start | bytes 2621440 | tf_op jit(solution)/shard_map/all_gather | solution.py:129
  10.0 94.6 %all-gather.35.cloned.1.call-start = ((), (), s32[]{:S(2)}) async-start(), calls=%async_computation.1 | async-start | bytes 2621440 | tf_op jit(solution)/shard_map/all_gather | solution.py:129
  11.2 139.5 %all-gather.37.cloned.1.call-start = ((), (), s32[]{:S(2)}) async-start(), calls=%async_computation.2 | async-start | bytes 2621440 | tf_op jit(solution)/shard_map/all_gather | solution.py:129
  12.4 184.2 %all-gather.41.cloned.1.call-start = ((), (), s32[]{:S(2)}) async-start(), calls=%async_computation.4 | async-start | bytes 2621440 | tf_op jit(solution)/shard_map/all_gather | solution.py:129
  13.6 265.8 %all-gather.39.cloned.1.call-start = ((), (), s32[]{:S(2)}) async-start(), calls=%async_computation.3 | async-start | bytes 2621440 | tf_op jit(solution)/shard_map/all_gather | solution.py:129
  61.3 47.9 %collective-permute-start = (f32[2,2,32,2048]{3,2,1,0:T(8,128)}, f32[2,2,32,2048]{3,2,1,0:T(8,128)S(1)}, u32[]{:S(2)}, u32[]{:S(2)}) collective-permute-start(f32[2,2,32,2048]{3,2,1,0:T(8,128)} %get-tuple-element.117), channel_id=1, source_target_pairs={{0,4},{4,0},{1,5},{5,1},{2,6},{6,2},{3,7},{7,3},{8,12},{12,8},{9,1... | collective-permute-start | bytes 3145736 | tf_op jit(solution)/shard_map/ppermute | solution.py:136
  107.7 49.6 %collective-permute-start.5 = (f32[2,2,32,2048]{3,2,1,0:T(8,128)}, f32[2,2,32,2048]{3,2,1,0:T(8,128)}, u32[]{:S(2)}, u32[]{:S(2)}) collective-permute-start(f32[2,2,32,2048]{3,2,1,0:T(8,128)} %get-tuple-element.116.refs_3_), channel_id=1, source_target_pairs={{0,4},{4,0},{1,5},{5,1},{2,6},{6,2},{3,7},{7,3},{8,12},{12,8},{9,1... | collective-permute-start | bytes 3145736 | tf_op jit(solution)/shard_map/ppermute | solution.py:136
  188.9 148.0 %all-gather.43.cloned.1.call-start = ((), (), s32[]{:S(2)}) async-start(), calls=%async_computation.5 | async-start | bytes 2621440 | tf_op jit(solution)/shard_map/all_gather | solution.py:129
  188.9 41.4 %collective-permute-start.11 = (f32[2,2,32,2048]{3,2,1,0:T(8,128)}, f32[2,2,32,2048]{3,2,1,0:T(8,128)}, u32[]{:S(2)}, u32[]{:S(2)}) collective-permute-start(f32[2,2,32,2048]{3,2,1,0:T(8,128)} %copy-done.17), channel_id=1, source_target_pairs={{0,4},{4,0},{1,5},{5,1},{2,6},{6,2},{3,7},{7,3},{8,12},{12,8},{9,1... | collective-permute-start | bytes 3145736 | tf_op jit(solution)/shard_map/ppermute | solution.py:136
  261.7 158.3 %all-gather.45.cloned.1.call-start = ((), (), s32[]{:S(2)}) async-start(), calls=%async_computation.6 | async-start | bytes 2621440 | tf_op jit(solution)/shard_map/all_gather | solution.py:129
  277.5 50.7 %collective-permute-start.17 = (f32[2,32,2048]{2,1,0:T(8,128)S(1)}, f32[2,32,2048]{2,1,0:T(8,128)}, u32[]{:S(2)}, u32[]{:S(2)}) collective-permute-start(f32[2,32,2048]{2,1,0:T(8,128)S(1)} %add_add_fusion.13.refs_4_.refs_1_), channel_id=1, source_target_pairs={{0,8},{8,0},{16,24},{24,16},{1,9},{9,1},{17,25},{25,17},{2,10},{10... | collective-permute-start | bytes 1572872 | tf_op jit(solution)/shard_map/ppermute | solution.py:151
  277.5 50.7 %collective-permute-start.18 = (f32[2,32,2048]{2,1,0:T(8,128)S(1)}, f32[2,32,2048]{2,1,0:T(8,128)}, u32[]{:S(2)}, u32[]{:S(2)}) collective-permute-start(f32[2,32,2048]{2,1,0:T(8,128)S(1)} %add_add_fusion.13.refs_4_.refs_1_), channel_id=1, source_target_pairs={{0,16},{8,24},{16,0},{24,8},{1,17},{9,25},{17,1},{25,9},{2,18},{10... | collective-permute-start | bytes 1572872 | tf_op jit(solution)/shard_map/ppermute | solution.py:151
  279.1 49.1 %collective-permute-start.19 = (f32[2,32,2048]{2,1,0:T(8,128)S(1)}, f32[2,32,2048]{2,1,0:T(8,128)}, u32[]{:S(2)}, u32[]{:S(2)}) collective-permute-start(f32[2,32,2048]{2,1,0:T(8,128)S(1)} %add_add_fusion.13.refs_4_.refs_1_), channel_id=1, source_target_pairs={{0,24},{8,16},{16,8},{24,0},{1,25},{9,17},{17,9},{25,1},{2,26},{10... | collective-permute-start | bytes 1572872 | tf_op jit(solution)/shard_map/ppermute | solution.py:151
  330.6 158.6 %all-gather.47.cloned.1.call-start = ((), (), s32[]{:S(2)}) async-start(), calls=%async_computation.7 | async-start | bytes 2621440 | tf_op jit(solution)/shard_map/all_gather | solution.py:129
  401.6 167.5 %all-gather.49.cloned.1.call-start = ((), (), s32[]{:S(2)}) async-start(), calls=%async_computation.8 | async-start | bytes 2621440 | tf_op jit(solution)/shard_map/all_gather | solution.py:129
  418.1 50.2 %collective-permute-start.27 = (f32[2,32,2048]{2,1,0:T(8,128)S(1)}, f32[2,32,2048]{2,1,0:T(8,128)}, u32[]{:S(2)}, u32[]{:S(2)}) collective-permute-start(f32[2,32,2048]{2,1,0:T(8,128)S(1)} %add_add_fusion.11.refs_4_.refs_1_), channel_id=1, source_target_pairs={{0,8},{8,0},{16,24},{24,16},{1,9},{9,1},{17,25},{25,17},{2,10},{10... | collective-permute-start | bytes 1572872 | tf_op jit(solution)/shard_map/ppermute | solution.py:151
  418.2 50.1 %collective-permute-start.28 = (f32[2,32,2048]{2,1,0:T(8,128)S(1)}, f32[2,32,2048]{2,1,0:T(8,128)}, u32[]{:S(2)}, u32[]{:S(2)}) collective-permute-start(f32[2,32,2048]{2,1,0:T(8,128)S(1)} %add_add_fusion.11.refs_4_.refs_1_), channel_id=1, source_target_pairs={{0,16},{8,24},{16,0},{24,8},{1,17},{9,25},{17,1},{25,9},{2,18},{10... | collective-permute-start | bytes 1572872 | tf_op jit(solution)/shard_map/ppermute | solution.py:151
  419.8 48.6 %collective-permute-start.29 = (f32[2,32,2048]{2,1,0:T(8,128)S(1)}, f32[2,32,2048]{2,1,0:T(8,128)}, u32[]{:S(2)}, u32[]{:S(2)}) collective-permute-start(f32[2,32,2048]{2,1,0:T(8,128)S(1)} %add_add_fusion.11.refs_4_.refs_1_), channel_id=1, source_target_pairs={{0,24},{8,16},{16,8},{24,0},{1,25},{9,17},{17,9},{25,1},{2,26},{10... | collective-permute-start | bytes 1572872 | tf_op jit(solution)/shard_map/ppermute | solution.py:151
  470.8 168.7 %all-gather.51.cloned.1.call-start = ((), (), s32[]{:S(2)}) async-start(), calls=%async_computation.9 | async-start | bytes 2621440 | tf_op jit(solution)/shard_map/all_gather | solution.py:129
  487.3 49.5 %collective-permute-start.32 = (f32[2,32,2048]{2,1,0:T(8,128)S(1)}, f32[2,32,2048]{2,1,0:T(8,128)S(1)}, u32[]{:S(2)}, u32[]{:S(2)}) collective-permute-start(f32[2,32,2048]{2,1,0:T(8,128)S(1)} %add_add_fusion.10.refs_4_.refs_1_), channel_id=1, source_target_pairs={{0,8},{8,0},{16,24},{24,16},{1,9},{9,1},{17,25},{25,17},{2,10},{10... | collective-permute-start | bytes 1572872 | tf_op jit(solution)/shard_map/ppermute | solution.py:151
  487.4 49.4 %collective-permute-start.33 = (f32[2,32,2048]{2,1,0:T(8,128)S(1)}, f32[2,32,2048]{2,1,0:T(8,128)}, u32[]{:S(2)}, u32[]{:S(2)}) collective-permute-start(f32[2,32,2048]{2,1,0:T(8,128)S(1)} %add_add_fusion.10.refs_4_.refs_1_), channel_id=1, source_target_pairs={{0,16},{8,24},{16,0},{24,8},{1,17},{9,25},{17,1},{25,9},{2,18},{10... | collective-permute-start | bytes 1572872 | tf_op jit(solution)/shard_map/ppermute | solution.py:151
  488.9 47.9 %collective-permute-start.34 = (f32[2,32,2048]{2,1,0:T(8,128)S(1)}, f32[2,32,2048]{2,1,0:T(8,128)}, u32[]{:S(2)}, u32[]{:S(2)}) collective-permute-start(f32[2,32,2048]{2,1,0:T(8,128)S(1)} %add_add_fusion.10.refs_4_.refs_1_), channel_id=1, source_target_pairs={{0,24},{8,16},{16,8},{24,0},{1,25},{9,17},{17,9},{25,1},{2,26},{10... | collective-permute-start | bytes 1572872 | tf_op jit(solution)/shard_map/ppermute | solution.py:151
  539.1 164.8 %all-gather.53.cloned.1.call-start = ((), (), s32[]{:S(2)}) async-start(), calls=%async_computation.10 | async-start | bytes 2621440 | tf_op jit(solution)/shard_map/all_gather | solution.py:129
  567.2 48.6 %collective-permute-start.40 = (f32[2,32,2048]{2,1,0:T(8,128)S(1)}, f32[2,32,2048]{2,1,0:T(8,128)S(1)}, u32[]{:S(2)}, u32[]{:S(2)}) collective-permute-start(f32[2,32,2048]{2,1,0:T(8,128)S(1)} %add_add_fusion.9.refs_4_.refs_1_), channel_id=1, source_target_pairs={{0,8},{8,0},{16,24},{24,16},{1,9},{9,1},{17,25},{25,17},{2,10},{10... | collective-permute-start | bytes 1572872 | tf_op jit(solution)/shard_map/ppermute | solution.py:151
  567.2 49.4 %collective-permute-start.41 = (f32[2,32,2048]{2,1,0:T(8,128)S(1)}, f32[2,32,2048]{2,1,0:T(8,128)}, u32[]{:S(2)}, u32[]{:S(2)}) collective-permute-start(f32[2,32,2048]{2,1,0:T(8,128)S(1)} %add_add_fusion.9.refs_4_.refs_1_), channel_id=1, source_target_pairs={{0,16},{8,24},{16,0},{24,8},{1,17},{9,25},{17,1},{25,9},{2,18},{10... | collective-permute-start | bytes 1572872 | tf_op jit(solution)/shard_map/ppermute | solution.py:151
  568.8 47.8 %collective-permute-start.42 = (f32[2,32,2048]{2,1,0:T(8,128)S(1)}, f32[2,32,2048]{2,1,0:T(8,128)}, u32[]{:S(2)}, u32[]{:S(2)}) collective-permute-start(f32[2,32,2048]{2,1,0:T(8,128)S(1)} %add_add_fusion.9.refs_4_.refs_1_), channel_id=1, source_target_pairs={{0,24},{8,16},{16,8},{24,0},{1,25},{9,17},{17,9},{25,1},{2,26},{10... | collective-permute-start | bytes 1572872 | tf_op jit(solution)/shard_map/ppermute | solution.py:151
  621.1 148.7 %all-gather.57.cloned.1.call-start = ((), (), s32[]{:S(2)}) async-start(), calls=%async_computation.12 | async-start | bytes 2621440 | tf_op jit(solution)/shard_map/all_gather | solution.py:129
  637.5 46.9 %collective-permute-start.49 = (f32[2,32,2048]{2,1,0:T(8,128)S(1)}, f32[2,32,2048]{2,1,0:T(8,128)}, u32[]{:S(2)}, u32[]{:S(2)}) collective-permute-start(f32[2,32,2048]{2,1,0:T(8,128)S(1)} %add_add_fusion.8.refs_4_.refs_1_), channel_id=1, source_target_pairs={{0,8},{8,0},{16,24},{24,16},{1,9},{9,1},{17,25},{25,17},{2,10},{10... | collective-permute-start | bytes 1572872 | tf_op jit(solution)/shard_map/ppermute | solution.py:151
  637.6 46.9 %collective-permute-start.50 = (f32[2,32,2048]{2,1,0:T(8,128)S(1)}, f32[2,32,2048]{2,1,0:T(8,128)}, u32[]{:S(2)}, u32[]{:S(2)}) collective-permute-start(f32[2,32,2048]{2,1,0:T(8,128)S(1)} %add_add_fusion.8.refs_4_.refs_1_), channel_id=1, source_target_pairs={{0,16},{8,24},{16,0},{24,8},{1,17},{9,25},{17,1},{25,9},{2,18},{10... | collective-permute-start | bytes 1572872 | tf_op jit(solution)/shard_map/ppermute | solution.py:151
  639.2 45.3 %collective-permute-start.51 = (f32[2,32,2048]{2,1,0:T(8,128)S(1)}, f32[2,32,2048]{2,1,0:T(8,128)}, u32[]{:S(2)}, u32[]{:S(2)}) collective-permute-start(f32[2,32,2048]{2,1,0:T(8,128)S(1)} %add_add_fusion.8.refs_4_.refs_1_), channel_id=1, source_target_pairs={{0,24},{8,16},{16,8},{24,0},{1,25},{9,17},{17,9},{25,1},{2,26},{10... | collective-permute-start | bytes 1572872 | tf_op jit(solution)/shard_map/ppermute | solution.py:151
  687.0 147.9 %all-gather.55.cloned.1.call-start = ((), (), s32[]{:S(2)}) async-start(), calls=%async_computation.11 | async-start | bytes 2621440 | tf_op jit(solution)/shard_map/all_gather | solution.py:129
  702.0 48.2 %collective-permute-start.36 = (f32[2,32,2048]{2,1,0:T(8,128)S(1)}, f32[2,32,2048]{2,1,0:T(8,128)}, u32[]{:S(2)}, u32[]{:S(2)}) collective-permute-start(f32[2,32,2048]{2,1,0:T(8,128)S(1)} %add_add_fusion.7.refs_4_.refs_1_), channel_id=1, source_target_pairs={{0,8},{8,0},{16,24},{24,16},{1,9},{9,1},{17,25},{25,17},{2,10},{10... | collective-permute-start | bytes 1572872 | tf_op jit(solution)/shard_map/ppermute | solution.py:151
  702.1 48.2 %collective-permute-start.37 = (f32[2,32,2048]{2,1,0:T(8,128)S(1)}, f32[2,32,2048]{2,1,0:T(8,128)}, u32[]{:S(2)}, u32[]{:S(2)}) collective-permute-start(f32[2,32,2048]{2,1,0:T(8,128)S(1)} %add_add_fusion.7.refs_4_.refs_1_), channel_id=1, source_target_pairs={{0,16},{8,24},{16,0},{24,8},{1,17},{9,25},{17,1},{25,9},{2,18},{10... | collective-permute-start | bytes 1572872 | tf_op jit(solution)/shard_map/ppermute | solution.py:151
  703.6 46.6 %collective-permute-start.38 = (f32[2,32,2048]{2,1,0:T(8,128)S(1)}, f32[2,32,2048]{2,1,0:T(8,128)}, u32[]{:S(2)}, u32[]{:S(2)}) collective-permute-start(f32[2,32,2048]{2,1,0:T(8,128)S(1)} %add_add_fusion.7.refs_4_.refs_1_), channel_id=1, source_target_pairs={{0,24},{8,16},{16,8},{24,0},{1,25},{9,17},{17,9},{25,1},{2,26},{10... | collective-permute-start | bytes 1572872 | tf_op jit(solution)/shard_map/ppermute | solution.py:151
  752.6 146.5 %all-gather.59.cloned.1.call-start = ((), (), s32[]{:S(2)}) async-start(), calls=%async_computation.13 | async-start | bytes 2621440 | tf_op jit(solution)/shard_map/all_gather | solution.py:129
  767.9 47.4 %collective-permute-start.45 = (f32[2,32,2048]{2,1,0:T(8,128)S(1)}, f32[2,32,2048]{2,1,0:T(8,128)}, u32[]{:S(2)}, u32[]{:S(2)}) collective-permute-start(f32[2,32,2048]{2,1,0:T(8,128)S(1)} %add_add_fusion.6.refs_4_.refs_1_), channel_id=1, source_target_pairs={{0,8},{8,0},{16,24},{24,16},{1,9},{9,1},{17,25},{25,17},{2,10},{10... | collective-permute-start | bytes 1572872 | tf_op jit(solution)/shard_map/ppermute | solution.py:151
  768.0 47.3 %collective-permute-start.46 = (f32[2,32,2048]{2,1,0:T(8,128)S(1)}, f32[2,32,2048]{2,1,0:T(8,128)}, u32[]{:S(2)}, u32[]{:S(2)}) collective-permute-start(f32[2,32,2048]{2,1,0:T(8,128)S(1)} %add_add_fusion.6.refs_4_.refs_1_), channel_id=1, source_target_pairs={{0,16},{8,24},{16,0},{24,8},{1,17},{9,25},{17,1},{25,9},{2,18},{10... | collective-permute-start | bytes 1572872 | tf_op jit(solution)/shard_map/ppermute | solution.py:151
  769.5 45.8 %collective-permute-start.47 = (f32[2,32,2048]{2,1,0:T(8,128)S(1)}, f32[2,32,2048]{2,1,0:T(8,128)}, u32[]{:S(2)}, u32[]{:S(2)}) collective-permute-start(f32[2,32,2048]{2,1,0:T(8,128)S(1)} %add_add_fusion.6.refs_4_.refs_1_), channel_id=1, source_target_pairs={{0,24},{8,16},{16,8},{24,0},{1,25},{9,17},{17,9},{25,1},{2,26},{10... | collective-permute-start | bytes 1572872 | tf_op jit(solution)/shard_map/ppermute | solution.py:151
  817.8 143.1 %all-gather.61.cloned.1.call-start = ((), (), s32[]{:S(2)}) async-start(), calls=%async_computation.14 | async-start | bytes 2621440 | tf_op jit(solution)/shard_map/all_gather | solution.py:129
  833.0 46.6 %collective-permute-start.57 = (f32[2,32,2048]{2,1,0:T(8,128)S(1)}, f32[2,32,2048]{2,1,0:T(8,128)}, u32[]{:S(2)}, u32[]{:S(2)}) collective-permute-start(f32[2,32,2048]{2,1,0:T(8,128)S(1)} %add_add_fusion.5.refs_4_.refs_1_), channel_id=1, source_target_pairs={{0,8},{8,0},{16,24},{24,16},{1,9},{9,1},{17,25},{25,17},{2,10},{10... | collective-permute-start | bytes 1572872 | tf_op jit(solution)/shard_map/ppermute | solution.py:151
  833.1 46.5 %collective-permute-start.58 = (f32[2,32,2048]{2,1,0:T(8,128)S(1)}, f32[2,32,2048]{2,1,0:T(8,128)}, u32[]{:S(2)}, u32[]{:S(2)}) collective-permute-start(f32[2,32,2048]{2,1,0:T(8,128)S(1)} %add_add_fusion.5.refs_4_.refs_1_), channel_id=1, source_target_pairs={{0,16},{8,24},{16,0},{24,8},{1,17},{9,25},{17,1},{25,9},{2,18},{10... | collective-permute-start | bytes 1572872 | tf_op jit(solution)/shard_map/ppermute | solution.py:151
  834.7 44.9 %collective-permute-start.59 = (f32[2,32,2048]{2,1,0:T(8,128)S(1)}, f32[2,32,2048]{2,1,0:T(8,128)}, u32[]{:S(2)}, u32[]{:S(2)}) collective-permute-start(f32[2,32,2048]{2,1,0:T(8,128)S(1)} %add_add_fusion.5.refs_4_.refs_1_), channel_id=1, source_target_pairs={{0,24},{8,16},{16,8},{24,0},{1,25},{9,17},{17,9},{25,1},{2,26},{10... | collective-permute-start | bytes 1572872 | tf_op jit(solution)/shard_map/ppermute | solution.py:151
  882.0 138.7 %all-gather.63.cloned.1.call-start = ((), (), s32[]{:S(2)}) async-start(), calls=%async_computation.15 | async-start | bytes 2621440 | tf_op jit(solution)/shard_map/all_gather | solution.py:129
  897.2 46.0 %collective-permute-start.62 = (f32[2,32,2048]{2,1,0:T(8,128)S(1)}, f32[2,32,2048]{2,1,0:T(8,128)}, u32[]{:S(2)}, u32[]{:S(2)}) collective-permute-start(f32[2,32,2048]{2,1,0:T(8,128)S(1)} %add_add_fusion.4.refs_4_.refs_1_), channel_id=1, source_target_pairs={{0,8},{8,0},{16,24},{24,16},{1,9},{9,1},{17,25},{25,17},{2,10},{10... | collective-permute-start | bytes 1572872 | tf_op jit(solution)/shard_map/ppermute | solution.py:151
  897.3 45.9 %collective-permute-start.63 = (f32[2,32,2048]{2,1,0:T(8,128)S(1)}, f32[2,32,2048]{2,1,0:T(8,128)}, u32[]{:S(2)}, u32[]{:S(2)}) collective-permute-start(f32[2,32,2048]{2,1,0:T(8,128)S(1)} %add_add_fusion.4.refs_4_.refs_1_), channel_id=1, source_target_pairs={{0,16},{8,24},{16,0},{24,8},{1,17},{9,25},{17,1},{25,9},{2,18},{10... | collective-permute-start | bytes 1572872 | tf_op jit(solution)/shard_map/ppermute | solution.py:151
  898.9 44.2 %collective-permute-start.64 = (f32[2,32,2048]{2,1,0:T(8,128)S(1)}, f32[2,32,2048]{2,1,0:T(8,128)}, u32[]{:S(2)}, u32[]{:S(2)}) collective-permute-start(f32[2,32,2048]{2,1,0:T(8,128)S(1)} %add_add_fusion.4.refs_4_.refs_1_), channel_id=1, source_target_pairs={{0,24},{8,16},{16,8},{24,0},{1,25},{9,17},{17,9},{25,1},{2,26},{10... | collective-permute-start | bytes 1572872 | tf_op jit(solution)/shard_map/ppermute | solution.py:151
  1022.6 58.0 %collective-permute-start.66 = (f32[2,2,32,2048]{3,2,1,0:T(8,128)S(1)}, f32[2,2,32,2048]{3,2,1,0:T(8,128)S(1)}, u32[]{:S(2)}, u32[]{:S(2)}) collective-permute-start(f32[2,2,32,2048]{3,2,1,0:T(8,128)S(1)} %get-tuple-element.85.refs_3_), channel_id=1, source_target_pairs={{0,4},{4,0},{1,5},{5,1},{2,6},{6,2},{3,7},{7,3},{8,12},{12,8},{9,1... | collective-permute-start | bytes 3145736 | tf_op jit(solution)/shard_map/ppermute | solution.py:136
  1136.9 43.6 %collective-permute-start.79 = (f32[2,32,2048]{2,1,0:T(8,128)S(1)}, f32[2,32,2048]{2,1,0:T(8,128)}, u32[]{:S(2)}, u32[]{:S(2)}) collective-permute-start(f32[2,32,2048]{2,1,0:T(8,128)S(1)} %add_add_fusion.refs_1_), channel_id=1, source_target_pairs={{0,24},{8,16},{16,8},{24,0},{1,25},{9,17},{17,9},{25,1},{2,26},{10... | collective-permute-start | bytes 1572872 | tf_op jit(solution)/shard_map/ppermute | solution.py:151
  (112 other events, 2508.6 us)
Sparse Core Ops, SparseCore 0:
  10.1 48.3 all-gather.32
  60.1 44.4 all-gather.34
  106.2 44.4 all-gather.36
  152.1 44.4 all-gather.40
  198.0 44.4 all-gather.38
  261.8 44.4 all-gather.42
  330.8 44.4 all-gather.44
  401.7 44.5 all-gather.46
  470.9 44.4 all-gather.48
  539.2 44.4 all-gather.50
  621.2 44.4 all-gather.52
  687.1 44.4 all-gather.56
  752.8 44.5 all-gather.54
  817.9 44.5 all-gather.58
  882.1 44.5 all-gather.60
  945.8 44.5 all-gather.62

commit v2 on v1

--- a/solution.py
+++ b/solution.py
@@ -175,13 +175,17 @@
         energy = convolution(weights[block][chunk], masks, blocks, ties)
         if step[:2] == steps[-1][:2]:
             energies[chunk] = energy
+            done.append(energy)
         else:
             spreads[chunk] = relayout(energy)
 
+    done = []
     waiting = None
     for position, step in enumerate(steps):
         block, sweep, chunk = step
-        ties = []
+        ties = list(done[-1:])
+        if position == 0:
+            ties += [weight for block_weights in weights for weight in block_weights]
         if position + 1 < len(steps):
             ties += spreads[steps[position + 1][2]][1]
         if waiting is not None:

time: 1200 us -> 1180 us (0.983)
  waiting for transfers between devices: 473 us -> 449 us
  starting transfers between devices: 80.2 us -> 65.4 us
  other arithmetic: 11.9 us -> 24.5 us
    ppermute x16, waiting for transfers between devices: 189 us -> 210 us  [reduce_rows(): total = total + lax.ppermute(partial[shift], 'tr', ring(-shift))]
    ppermute x48, waiting for transfers between devices: 44.5 us -> 27.1 us  [spread(): blocks.append(lax.ppermute(green, 'mom', swap))]
    all_gather x16, waiting for transfers between devices: 84.8 us -> 69.4 us  [relayout(): every = lax.all_gather(energy, 'tc', axis=0)]
    unnamed x143 -> x171, local copies, waits for them, and re-layouts: 58.5 us -> 43.9 us
    pallas_call x16, Pallas kernels: 464 us -> 477 us  [product(): pl.pallas_call(functools.partial(product_kernel, count, len(ties)), grid=...]
    ppermute x16, waiting for transfers between devices: 154 us -> 142 us  [relayout(): parts.append(lax.ppermute(sent[shift - 1], 'tr', ring(shift)))]
    dynamic_slice x10 -> x11, local copies, waits for them, and re-layouts: 29 us -> 29.5 us  [relayout(): parts = [lax.dynamic_slice_in_dim(every, own_split * pieces, pieces, 0)]]
  transfers between devices with their start and end apart: 96 -> 96, of which waited for: 36 -> 34; matrix products, arithmetic and copies ran while one was open for 9% -> 9% of each run, Pallas kernels for 41% -> 41%
where the time goes in v2:
time: 1180 us; the launch traced here: 1170 us
  Pallas kernels  505 us (43%)
  waiting for transfers between devices  449 us (38%)
  local copies, waits for them, and re-layouts  110 us (9%)
  starting transfers between devices  65.4 us (6%)
  other arithmetic  24.5 us (2%)
  between operations  15.3 us (1%)
    pallas_call x16, Pallas kernels, product(): pl.pallas_call(functools.partial(product_kernel, count, len(ties)), grid=...  477 us
    ppermute x16, waiting for transfers between devices, reduce_rows(): total = total + lax.ppermute(partial[shift], 'tr', ring(-shift))  210 us
    ppermute x16, waiting for transfers between devices, relayout(): parts.append(lax.ppermute(sent[shift - 1], 'tr', ring(shift)))  142 us
    all_gather x16, waiting for transfers between devices, relayout(): every = lax.all_gather(energy, 'tc', axis=0)  69.4 us
    unnamed x171, local copies, waits for them, and re-layouts  43.9 us
    ppermute x48, starting transfers between devices, spread(): blocks.append(lax.ppermute(green, 'mom', swap))  30.7 us
    dynamic_slice x11, local copies, waits for them, and re-layouts, relayout(): parts = [lax.dynamic_slice_in_dim(every, own_split * pieces, pieces, 0)]  29.5 us
    pallas_call x16, Pallas kernels, convolution(): pl.pallas_call(functools.partial(convolve_kernel, masks), grid=(columns /...  28.7 us
  transfers between devices with their start and end apart: 96, of which 34 were waited for; matrix products, arithmetic and copies ran while one was open for 9% of the time, Pallas kernels for 41%

profile of v2, /device:TPU:0, one launch (start us, length us, event | category | flops | bytes accessed | tf_op | source)
XLA Modules:
  0.0 1169.3 jit_solution(15557293730578659268)
XLA Ops:
  13.7 12.3 %fusion = (f32[1,32,8,2048]{3,2,1,0:T(8,128)}, f32[1,32,8,2048]{3,2,1,0:T(8,128)}, f32[1,32,8,2048]{3,2,1,0:T(8,128)}, f32[1,32,8,2048]{3,2,1,0:T(8,128)}, f32[1...) fusion(f32[2,128,8,2048]{3,2,1,0:T(8,128)} %param.7), kind=kLoop, calls=%fused_computation.67 | loop fusion | bytes 33554432 | tf_op jit(solution)/shard_map/slice | solution.py:155
  26.0 32.6 %all-gather.33.cloned.1.call-done = f32[8,32,2048]{2,1,0:T(8,128)} async-done(((f32[2,32,2048]{2,1,0:T(8,128)}), f32[8,32,2048]{2,1,0:T(8,128)}) %all-gather.33.cloned.1.call-update) | async-done | bytes 2097168 | tf_op jit(solution)/shard_map/all_gather | solution.py:129
  82.2 22.5 %all-gather.35.cloned.1.call-done = f32[8,32,2048]{2,1,0:T(8,128)} async-done(((f32[2,32,2048]{2,1,0:T(8,128)}), f32[8,32,2048]{2,1,0:T(8,128)}) %all-gather.35.cloned.1.call-update) | async-done | bytes 2097168 | tf_op jit(solution)/shard_map/all_gather | solution.py:129
  108.8 30.2 %shard_map.67 = (f32[2,32,2048]{2,1,0:T(8,128)S(1)}, f32[2,32,2048]{2,1,0:T(8,128)}) custom-call(f32[2,2,32,2048]{3,2,1,0:T(8,128)S(1)} %get-tuple-element.118.refs_0_, f32[2,2,32,2048]{3,2,1,0:T(8,128)S(1)} %collective-permute-done.refs_1_, f32[2,4096,2048]{2,1,0:T(8,128)} %refs_2_.31, f32[8,32,2048]{2,1,0:T(8,128)} %bitcast.109, f32[8,32,2048]{2,1,0:T(8,128)} %bitcast.106, ...), custom_call_target="tpu_custom_call" | custom-call | flops 6442450944 | bytes 67108864 | tf_op jit(solution)/shard_map/pallas_call | solution.py:61
  141.8 9.0 all-gather.37.cloned.1.call-done
  156.7 30.2 %shard_map.68 = (f32[2,32,2048]{2,1,0:T(8,128)S(1)}, f32[2,32,2048]{2,1,0:T(8,128)}) custom-call(f32[2,2,32,2048]{3,2,1,0:T(8,128)S(1)} %get-tuple-element.115.refs_0_, f32[2,2,32,2048]{3,2,1,0:T(8,128)} %collective-permute-done.5.refs_1_, f32[2,4096,2048]{2,1,0:T(8,128)} %refs_2_.31, f32[2,2,32,2048]{3,2,1,0:T(8,128)S(1)} %get-tuple-element.110.refs_3_, ...), custom_call_target="tpu_custom_call" | custom-call | flops 6442450944 | bytes 67108864 | tf_op jit(solution)/shard_map/pallas_call | solution.py:61
  198.5 27.6 %collective-permute-done.7 = f32[2,32,2048]{2,1,0:T(8,128)} collective-permute-done((f32[2,32,2048]{2,1,0:T(8,128)}, f32[2,32,2048]{2,1,0:T(8,128)}, u32[]{:S(2)}, u32[]{:S(2)}) %collective-permute-start.7) | collective-permute-done | bytes 524320 | tf_op jit(solution)/shard_map/ppermute | solution.py:142
  229.7 29.0 %shard_map.70 = (f32[2,32,2048]{2,1,0:T(8,128)S(1)}, f32[2,32,2048]{2,1,0:T(8,128)S(1)}) custom-call(f32[2,2,32,2048]{3,2,1,0:T(8,128)S(1)} %get-tuple-element.109.refs_0_, f32[2,2,32,2048]{3,2,1,0:T(8,128)} %collective-permute-done.11.refs_1_, f32[2,4096,2048]{2,1,0:T(8,128)} %refs_2_.31, f32[2,2,32,2048]{3,2,1,0:T(8,128)S(1)} %get-tuple-element.119.refs_3_, ...), custom_call_target="tpu_custom_call" | custom-call | flops 6442450944 | bytes 67108864 | tf_op jit(solution)/shard_map/pallas_call | solution.py:61
  263.9 12.8 %collective-permute-done.13 = f32[2,32,2048]{2,1,0:T(8,128)S(1)} collective-permute-done((f32[2,32,2048]{2,1,0:T(8,128)S(1)}, f32[2,32,2048]{2,1,0:T(8,128)S(1)}, u32[]{:S(2)}, u32[]{:S(2)}) %collective-permute-start.13) | collective-permute-done | bytes 524320 | tf_op jit(solution)/shard_map/ppermute | solution.py:142
  282.8 15.3 %collective-permute-done.12.refs_1_ = f32[2,2,32,2048]{3,2,1,0:T(8,128)} collective-permute-done((f32[2,2,32,2048]{3,2,1,0:T(8,128)S(1)}, f32[2,2,32,2048]{3,2,1,0:T(8,128)}, u32[]{:S(2)}, u32[]{:S(2)}) %collective-permute-start.12) | collective-permute-done | bytes 1048608 | tf_op jit(solution)/shard_map/ppermute | solution.py:136
  298.0 29.0 %shard_map.72 = (f32[2,32,2048]{2,1,0:T(8,128)S(1)}, f32[2,32,2048]{2,1,0:T(8,128)S(1)}) custom-call(f32[2,2,32,2048]{3,2,1,0:T(8,128)S(1)} %get-tuple-element.120.refs_0_, f32[2,2,32,2048]{3,2,1,0:T(8,128)} %collective-permute-done.12.refs_1_, f32[2,4096,2048]{2,1,0:T(8,128)} %refs_2_.31, f32[2,2,32,2048]{3,2,1,0:T(8,128)S(1)} %get-tuple-element.104.refs_3_, ...), custom_call_target="tpu_custom_call" | custom-call | flops 6442450944 | bytes 67108864 | tf_op jit(solution)/shard_map/pallas_call | solution.py:61
  336.6 29.9 %collective-permute-done.14 = f32[2,32,2048]{2,1,0:T(8,128)S(1)} collective-permute-done((f32[2,32,2048]{2,1,0:T(8,128)S(1)}, f32[2,32,2048]{2,1,0:T(8,128)S(1)}, u32[]{:S(2)}, u32[]{:S(2)}) %collective-permute-start.14) | collective-permute-done | bytes 524320 | tf_op jit(solution)/shard_map/ppermute | solution.py:142
  368.8 29.1 %shard_map.73 = (f32[2,32,2048]{2,1,0:T(8,128)S(1)}, f32[2,32,2048]{2,1,0:T(8,128)S(1)}) custom-call(f32[2,2,32,2048]{3,2,1,0:T(8,128)S(1)} %copy-done.19, f32[2,2,32,2048]{3,2,1,0:T(8,128)} %collective-permute-done.6.refs_1_, f32[2,4096,2048]{2,1,0:T(8,128)} %refs_2_.31, f32[2,2,32,2048]{3,2,1,0:T(8,128)} %get-tuple-element.100.refs_3_, ...), custom_call_target="tpu_custom_call" | custom-call | flops 6442450944 | bytes 67108864 | tf_op jit(solution)/shard_map/pallas_call | solution.py:61
  402.4 13.0 %collective-permute-done.15 = f32[2,32,2048]{2,1,0:T(8,128)S(1)} collective-permute-done((f32[2,32,2048]{2,1,0:T(8,128)}, f32[2,32,2048]{2,1,0:T(8,128)S(1)}, u32[]{:S(2)}, u32[]{:S(2)}) %collective-permute-start.15) | collective-permute-done | bytes 524320 | tf_op jit(solution)/shard_map/ppermute | solution.py:142
  421.5 15.8 %collective-permute-done.16.refs_1_ = f32[2,2,32,2048]{3,2,1,0:T(8,128)} collective-permute-done((f32[2,2,32,2048]{3,2,1,0:T(8,128)}, f32[2,2,32,2048]{3,2,1,0:T(8,128)}, u32[]{:S(2)}, u32[]{:S(2)}) %collective-permute-start.16) | collective-permute-done | bytes 1048608 | tf_op jit(solution)/shard_map/ppermute | solution.py:136
  437.3 39.2 %shard_map.75 = (f32[2,32,2048]{2,1,0:T(8,128)S(1)}, f32[2,32,2048]{2,1,0:T(8,128)S(1)}) custom-call(f32[2,2,32,2048]{3,2,1,0:T(8,128)S(1)} %copy-done.16, f32[2,2,32,2048]{3,2,1,0:T(8,128)} %collective-permute-done.16.refs_1_, f32[2,4096,2048]{2,1,0:T(8,128)} %refs_2_.31, f32[2,2,32,2048]{3,2,1,0:T(8,128)S(1)} %get-tuple-element.98.refs_3_, ...), custom_call_target="tpu_custom_call" | custom-call | flops 6442450944 | bytes 67108864 | tf_op jit(solution)/shard_map/pallas_call | solution.py:61
  482.6 13.0 %collective-permute-done.20 = f32[2,32,2048]{2,1,0:T(8,128)S(1)} collective-permute-done((f32[2,32,2048]{2,1,0:T(8,128)}, f32[2,32,2048]{2,1,0:T(8,128)S(1)}, u32[]{:S(2)}, u32[]{:S(2)}) %collective-permute-start.20) | collective-permute-done | bytes 524320 | tf_op jit(solution)/shard_map/ppermute | solution.py:142
  501.9 14.8 %collective-permute-done.21.refs_1_ = f32[2,2,32,2048]{3,2,1,0:T(8,128)} collective-permute-done((f32[2,2,32,2048]{3,2,1,0:T(8,128)}, f32[2,2,32,2048]{3,2,1,0:T(8,128)}, u32[]{:S(2)}, u32[]{:S(2)}) %collective-permute-start.21) | collective-permute-done | bytes 1048608 | tf_op jit(solution)/shard_map/ppermute | solution.py:136
  516.7 29.0 %shard_map.77 = (f32[2,32,2048]{2,1,0:T(8,128)S(1)}, f32[2,32,2048]{2,1,0:T(8,128)S(1)}) custom-call(f32[2,2,32,2048]{3,2,1,0:T(8,128)S(1)} %copy-done.20, f32[2,2,32,2048]{3,2,1,0:T(8,128)} %collective-permute-done.21.refs_1_, f32[2,4096,2048]{2,1,0:T(8,128)} %refs_2_.31, f32[2,2,32,2048]{3,2,1,0:T(8,128)S(1)} %get-tuple-element.101.refs_3_, ...), custom_call_target="tpu_custom_call" | custom-call | flops 6442450944 | bytes 67108864 | tf_op jit(solution)/shard_map/pallas_call | solution.py:61
  552.0 13.0 %collective-permute-done.25 = f32[2,32,2048]{2,1,0:T(8,128)S(1)} collective-permute-done((f32[2,32,2048]{2,1,0:T(8,128)}, f32[2,32,2048]{2,1,0:T(8,128)S(1)}, u32[]{:S(2)}, u32[]{:S(2)}) %collective-permute-start.25) | collective-permute-done | bytes 524320 | tf_op jit(solution)/shard_map/ppermute | solution.py:142
  572.1 13.1 %collective-permute-done.26.refs_1_ = f32[2,2,32,2048]{3,2,1,0:T(8,128)} collective-permute-done((f32[2,2,32,2048]{3,2,1,0:T(8,128)}, f32[2,2,32,2048]{3,2,1,0:T(8,128)}, u32[]{:S(2)}, u32[]{:S(2)}) %collective-permute-start.26) | collective-permute-done | bytes 1048608 | tf_op jit(solution)/shard_map/ppermute | solution.py:136
  585.2 29.1 %shard_map.79 = (f32[2,32,2048]{2,1,0:T(8,128)S(1)}, f32[2,32,2048]{2,1,0:T(8,128)S(1)}) custom-call(f32[2,2,32,2048]{3,2,1,0:T(8,128)S(1)} %copy-done.21, f32[2,2,32,2048]{3,2,1,0:T(8,128)} %collective-permute-done.26.refs_1_, f32[2,4096,2048]{2,1,0:T(8,128)} %refs_2_.31, f32[2,2,32,2048]{3,2,1,0:T(8,128)S(1)} %get-tuple-element.96.refs_3_, ...), custom_call_target="tpu_custom_call" | custom-call | flops 6442450944 | bytes 67108864 | tf_op jit(solution)/shard_map/pallas_call | solution.py:61
  620.7 13.0 %collective-permute-done.30 = f32[2,32,2048]{2,1,0:T(8,128)S(1)} collective-permute-done((f32[2,32,2048]{2,1,0:T(8,128)}, f32[2,32,2048]{2,1,0:T(8,128)S(1)}, u32[]{:S(2)}, u32[]{:S(2)}) %collective-permute-start.30) | collective-permute-done | bytes 524320 | tf_op jit(solution)/shard_map/ppermute | solution.py:142
  640.8 12.3 %collective-permute-done.31.refs_1_ = f32[2,2,32,2048]{3,2,1,0:T(8,128)} collective-permute-done((f32[2,2,32,2048]{3,2,1,0:T(8,128)}, f32[2,2,32,2048]{3,2,1,0:T(8,128)}, u32[]{:S(2)}, u32[]{:S(2)}) %collective-permute-start.31) | collective-permute-done | bytes 1048608 | tf_op jit(solution)/shard_map/ppermute | solution.py:136
  653.0 28.9 %shard_map.81 = (f32[2,32,2048]{2,1,0:T(8,128)S(1)}, f32[2,32,2048]{2,1,0:T(8,128)S(1)}) custom-call(f32[2,2,32,2048]{3,2,1,0:T(8,128)S(1)} %copy-done.22, f32[2,2,32,2048]{3,2,1,0:T(8,128)} %collective-permute-done.31.refs_1_, f32[2,4096,2048]{2,1,0:T(8,128)} %refs_2_.31, f32[2,2,32,2048]{3,2,1,0:T(8,128)S(1)} %get-tuple-element.92.refs_3_, ...), custom_call_target="tpu_custom_call" | custom-call | flops 6442450944 | bytes 67108864 | tf_op jit(solution)/shard_map/pallas_call | solution.py:61
  688.4 13.0 %collective-permute-done.35 = f32[2,32,2048]{2,1,0:T(8,128)S(1)} collective-permute-done((f32[2,32,2048]{2,1,0:T(8,128)}, f32[2,32,2048]{2,1,0:T(8,128)S(1)}, u32[]{:S(2)}, u32[]{:S(2)}) %collective-permute-start.35) | collective-permute-done | bytes 524320 | tf_op jit(solution)/shard_map/ppermute | solution.py:142
  706.3 13.6 %collective-permute-done.39.refs_1_ = f32[2,2,32,2048]{3,2,1,0:T(8,128)} collective-permute-done((f32[2,2,32,2048]{3,2,1,0:T(8,128)}, f32[2,2,32,2048]{3,2,1,0:T(8,128)}, u32[]{:S(2)}, u32[]{:S(2)}) %collective-permute-start.39) | collective-permute-done | bytes 1048608 | tf_op jit(solution)/shard_map/ppermute | solution.py:136
  719.9 29.0 %shard_map.83 = (f32[2,32,2048]{2,1,0:T(8,128)S(1)}, f32[2,32,2048]{2,1,0:T(8,128)S(1)}) custom-call(f32[2,2,32,2048]{3,2,1,0:T(8,128)S(1)} %copy-done.23, f32[2,2,32,2048]{3,2,1,0:T(8,128)} %collective-permute-done.39.refs_1_, f32[2,4096,2048]{2,1,0:T(8,128)} %refs_2_.31, f32[2,2,32,2048]{3,2,1,0:T(8,128)S(1)} %get-tuple-element.90.refs_3_, ...), custom_call_target="tpu_custom_call" | custom-call | flops 6442450944 | bytes 67108864 | tf_op jit(solution)/shard_map/pallas_call | solution.py:61
  754.3 13.0 %collective-permute-done.44 = f32[2,32,2048]{2,1,0:T(8,128)S(1)} collective-permute-done((f32[2,32,2048]{2,1,0:T(8,128)}, f32[2,32,2048]{2,1,0:T(8,128)S(1)}, u32[]{:S(2)}, u32[]{:S(2)}) %collective-permute-start.44) | collective-permute-done | bytes 524320 | tf_op jit(solution)/shard_map/ppermute | solution.py:142
  772.0 12.9 %collective-permute-done.48.refs_1_ = f32[2,2,32,2048]{3,2,1,0:T(8,128)} collective-permute-done((f32[2,2,32,2048]{3,2,1,0:T(8,128)}, f32[2,2,32,2048]{3,2,1,0:T(8,128)}, u32[]{:S(2)}, u32[]{:S(2)}) %collective-permute-start.48) | collective-permute-done | bytes 1048608 | tf_op jit(solution)/shard_map/ppermute | solution.py:136
  784.9 29.0 %shard_map.86 = (f32[2,32,2048]{2,1,0:T(8,128)S(1)}, f32[2,32,2048]{2,1,0:T(8,128)S(1)}) custom-call(f32[2,2,32,2048]{3,2,1,0:T(8,128)S(1)} %get-tuple-element.89.refs_0_, f32[2,2,32,2048]{3,2,1,0:T(8,128)} %collective-permute-done.48.refs_1_, f32[2,4096,2048]{2,1,0:T(8,128)} %refs_2_.31, f32[2,2,32,2048]{3,2,1,0:T(8,128)S(1)} %get-tuple-element.93.refs_3_, ...), custom_call_target="tpu_custom_call" | custom-call | flops 6442450944 | bytes 67108864 | tf_op jit(solution)/shard_map/pallas_call | solution.py:61
  819.4 13.0 %collective-permute-done.53 = f32[2,32,2048]{2,1,0:T(8,128)S(1)} collective-permute-done((f32[2,32,2048]{2,1,0:T(8,128)}, f32[2,32,2048]{2,1,0:T(8,128)S(1)}, u32[]{:S(2)}, u32[]{:S(2)}) %collective-permute-start.53) | collective-permute-done | bytes 524320 | tf_op jit(solution)/shard_map/ppermute | solution.py:142
  838.2 10.9 collective-permute-done.52.refs_1_
  849.2 29.0 %shard_map.88 = (f32[2,32,2048]{2,1,0:T(8,128)S(1)}, f32[2,32,2048]{2,1,0:T(8,128)S(1)}) custom-call(f32[2,2,32,2048]{3,2,1,0:T(8,128)S(1)} %copy-done.24, f32[2,2,32,2048]{3,2,1,0:T(8,128)} %collective-permute-done.52.refs_1_, f32[2,4096,2048]{2,1,0:T(8,128)} %refs_2_.31, f32[2,2,32,2048]{3,2,1,0:T(8,128)S(1)} %get-tuple-element.88.refs_3_, ...), custom_call_target="tpu_custom_call" | custom-call | flops 6442450944 | bytes 67108864 | tf_op jit(solution)/shard_map/pallas_call | solution.py:61
  883.6 13.0 %collective-permute-done.54 = f32[2,32,2048]{2,1,0:T(8,128)S(1)} collective-permute-done((f32[2,32,2048]{2,1,0:T(8,128)}, f32[2,32,2048]{2,1,0:T(8,128)S(1)}, u32[]{:S(2)}, u32[]{:S(2)}) %collective-permute-start.54) | collective-permute-done | bytes 524320 | tf_op jit(solution)/shard_map/ppermute | solution.py:142
  903.2 9.4 collective-permute-done.43.refs_1_
  912.6 29.3 %shard_map.89 = (f32[2,32,2048]{2,1,0:T(8,128)S(1)}, f32[2,32,2048]{2,1,0:T(8,128)S(1)}) custom-call(f32[2,2,32,2048]{3,2,1,0:T(8,128)S(1)} %copy-done.25, f32[2,2,32,2048]{3,2,1,0:T(8,128)} %collective-permute-done.43.refs_1_, f32[2,4096,2048]{2,1,0:T(8,128)} %refs_2_.31, f32[2,2,32,2048]{3,2,1,0:T(8,128)S(1)} %get-tuple-element.84.refs_3_, ...), custom_call_target="tpu_custom_call" | custom-call | flops 6442450944 | bytes 67108864 | tf_op jit(solution)/shard_map/pallas_call | solution.py:61
  948.3 13.0 %collective-permute-done.55 = f32[2,32,2048]{2,1,0:T(8,128)S(1)} collective-permute-done((f32[2,32,2048]{2,1,0:T(8,128)}, f32[2,32,2048]{2,1,0:T(8,128)S(1)}, u32[]{:S(2)}, u32[]{:S(2)}) %collective-permute-start.55) | collective-permute-done | bytes 524320 | tf_op jit(solution)/shard_map/ppermute | solution.py:142
  968.3 8.2 collective-permute-done.56.refs_1_
  976.5 29.1 %shard_map.91 = (f32[2,32,2048]{2,1,0:T(8,128)S(1)}, f32[2,32,2048]{2,1,0:T(8,128)S(1)}) custom-call(f32[2,2,32,2048]{3,2,1,0:T(8,128)S(1)} %copy-done.26, f32[2,2,32,2048]{3,2,1,0:T(8,128)} %collective-permute-done.56.refs_1_, f32[2,4096,2048]{2,1,0:T(8,128)} %refs_2_.31, f32[2,2,32,2048]{3,2,1,0:T(8,128)} %get-tuple-element.82.refs_3_, ...), custom_call_target="tpu_custom_call" | custom-call | flops 6442450944 | bytes 67108864 | tf_op jit(solution)/shard_map/pallas_call | solution.py:61
  1010.4 10.1 collective-permute-done.60
  1026.2 15.4 %collective-permute-done.61.refs_1_ = f32[2,2,32,2048]{3,2,1,0:T(8,128)} collective-permute-done((f32[2,2,32,2048]{3,2,1,0:T(8,128)}, f32[2,2,32,2048]{3,2,1,0:T(8,128)}, u32[]{:S(2)}, u32[]{:S(2)}) %collective-permute-start.61) | collective-permute-done | bytes 1048608 | tf_op jit(solution)/shard_map/ppermute | solution.py:136
  1041.6 29.1 %shard_map.94 = (f32[2,32,2048]{2,1,0:T(8,128)S(1)}, f32[2,32,2048]{2,1,0:T(8,128)S(1)}) custom-call(f32[2,2,32,2048]{3,2,1,0:T(8,128)S(1)} %copy-done.27, f32[2,2,32,2048]{3,2,1,0:T(8,128)} %collective-permute-done.61.refs_1_, f32[2,4096,2048]{2,1,0:T(8,128)} %refs_2_.31, f32[2,32,2048]{2,1,0:T(8,128)S(1)} %copy-done.15, ...), custom_call_target="tpu_custom_call" | custom-call | flops 6442450944 | bytes 67108864 | tf_op jit(solution)/shard_map/pallas_call | solution.py:61
  1081.1 28.6 %shard_map.96 = (f32[2,32,2048]{2,1,0:T(8,128)S(1)}, f32[2,32,2048]{2,1,0:T(8,128)S(1)}) custom-call(f32[2,2,32,2048]{3,2,1,0:T(8,128)S(1)} %get-tuple-element.86.refs_0_, f32[2,2,32,2048]{3,2,1,0:T(8,128)S(1)} %collective-permute-done.69.refs_1_, f32[2,4096,2048]{2,1,0:T(8,128)} %refs_2_.31, f32[2,32,2048]{2,1,0:T(8,128)S(1)} %shard_map.95.refs_3_, ...), custom_call_target="tpu_custom_call" | custom-call | flops 6442450944 | bytes 67108864 | tf_op jit(solution)/shard_map/pallas_call | solution.py:61
  1112.7 6.2 collective-permute-done.73
  1126.3 9.6 collective-permute-done.76.refs_4_
  1141.1 7.0 collective-permute-done.78.refs_3_
  1148.1 10.3 collective-permute-done.79.refs_4_
  (403 shorter events, 229.1 us)
Async XLA Ops:
  7.2 51.4 %all-gather.33.cloned.1.call-start = ((), (), s32[]{:S(2)}) async-start(), calls=%async_computation | async-start | bytes 2621440 | tf_op jit(solution)/shard_map/all_gather | solution.py:129
  10.1 94.6 %all-gather.35.cloned.1.call-start = ((), (), s32[]{:S(2)}) async-start(), calls=%async_computation.1 | async-start | bytes 2621440 | tf_op jit(solution)/shard_map/all_gather | solution.py:129
  11.3 139.5 %all-gather.37.cloned.1.call-start = ((), (), s32[]{:S(2)}) async-start(), calls=%async_computation.2 | async-start | bytes 2621440 | tf_op jit(solution)/shard_map/all_gather | solution.py:129
  12.4 184.2 %all-gather.41.cloned.1.call-start = ((), (), s32[]{:S(2)}) async-start(), calls=%async_computation.4 | async-start | bytes 2621440 | tf_op jit(solution)/shard_map/all_gather | solution.py:129
  13.6 266.4 %all-gather.39.cloned.1.call-start = ((), (), s32[]{:S(2)}) async-start(), calls=%async_computation.3 | async-start | bytes 2621440 | tf_op jit(solution)/shard_map/all_gather | solution.py:129
  61.5 47.3 %collective-permute-start = (f32[2,2,32,2048]{3,2,1,0:T(8,128)}, f32[2,2,32,2048]{3,2,1,0:T(8,128)S(1)}, u32[]{:S(2)}, u32[]{:S(2)}) collective-permute-start(f32[2,2,32,2048]{3,2,1,0:T(8,128)} %get-tuple-element.117), channel_id=1, source_target_pairs={{0,4},{4,0},{1,5},{5,1},{2,6},{6,2},{3,7},{7,3},{8,12},{12,8},{9,1... | collective-permute-start | bytes 3145736 | tf_op jit(solution)/shard_map/ppermute | solution.py:136
  107.4 49.3 %collective-permute-start.5 = (f32[2,2,32,2048]{3,2,1,0:T(8,128)}, f32[2,2,32,2048]{3,2,1,0:T(8,128)}, u32[]{:S(2)}, u32[]{:S(2)}) collective-permute-start(f32[2,2,32,2048]{3,2,1,0:T(8,128)} %get-tuple-element.116.refs_11_), channel_id=1, source_target_pairs={{0,4},{4,0},{1,5},{5,1},{2,6},{6,2},{3,7},{7,3},{8,12},{12,8},{9,1... | collective-permute-start | bytes 3145736 | tf_op jit(solution)/shard_map/ppermute | solution.py:136
  189.2 144.3 %all-gather.43.cloned.1.call-start = ((), (), s32[]{:S(2)}) async-start(), calls=%async_computation.5 | async-start | bytes 2621440 | tf_op jit(solution)/shard_map/all_gather | solution.py:129
  261.8 156.9 %all-gather.45.cloned.1.call-start = ((), (), s32[]{:S(2)}) async-start(), calls=%async_computation.6 | async-start | bytes 2621440 | tf_op jit(solution)/shard_map/all_gather | solution.py:129
  278.1 48.9 %collective-permute-start.17 = (f32[2,32,2048]{2,1,0:T(8,128)S(1)}, f32[2,32,2048]{2,1,0:T(8,128)S(1)}, u32[]{:S(2)}, u32[]{:S(2)}) collective-permute-start(f32[2,32,2048]{2,1,0:T(8,128)S(1)} %add_add_fusion.13.refs_4_.refs_1_), channel_id=1, source_target_pairs={{0,8},{8,0},{16,24},{24,16},{1,9},{9,1},{17,25},{25,17},{2,10},{10... | collective-permute-start | bytes 1572872 | tf_op jit(solution)/shard_map/ppermute | solution.py:151
  278.2 49.7 %collective-permute-start.18 = (f32[2,32,2048]{2,1,0:T(8,128)S(1)}, f32[2,32,2048]{2,1,0:T(8,128)}, u32[]{:S(2)}, u32[]{:S(2)}) collective-permute-start(f32[2,32,2048]{2,1,0:T(8,128)S(1)} %add_add_fusion.13.refs_4_.refs_1_), channel_id=1, source_target_pairs={{0,16},{8,24},{16,0},{24,8},{1,17},{9,25},{17,1},{25,9},{2,18},{10... | collective-permute-start | bytes 1572872 | tf_op jit(solution)/shard_map/ppermute | solution.py:151
  279.7 48.1 %collective-permute-start.19 = (f32[2,32,2048]{2,1,0:T(8,128)S(1)}, f32[2,32,2048]{2,1,0:T(8,128)}, u32[]{:S(2)}, u32[]{:S(2)}) collective-permute-start(f32[2,32,2048]{2,1,0:T(8,128)S(1)} %add_add_fusion.13.refs_4_.refs_1_), channel_id=1, source_target_pairs={{0,24},{8,16},{16,8},{24,0},{1,25},{9,17},{17,9},{25,1},{2,26},{10... | collective-permute-start | bytes 1572872 | tf_op jit(solution)/shard_map/ppermute | solution.py:151
  331.3 167.8 %all-gather.47.cloned.1.call-start = ((), (), s32[]{:S(2)}) async-start(), calls=%async_computation.7 | async-start | bytes 2621440 | tf_op jit(solution)/shard_map/all_gather | solution.py:129
  400.2 168.9 %all-gather.49.cloned.1.call-start = ((), (), s32[]{:S(2)}) async-start(), calls=%async_computation.8 | async-start | bytes 2621440 | tf_op jit(solution)/shard_map/all_gather | solution.py:129
  416.8 60.6 %collective-permute-start.27 = (f32[2,32,2048]{2,1,0:T(8,128)S(1)}, f32[2,32,2048]{2,1,0:T(8,128)S(1)}, u32[]{:S(2)}, u32[]{:S(2)}) collective-permute-start(f32[2,32,2048]{2,1,0:T(8,128)S(1)} %add_add_fusion.11.refs_4_.refs_1_), channel_id=1, source_target_pairs={{0,8},{8,0},{16,24},{24,16},{1,9},{9,1},{17,25},{25,17},{2,10},{10... | collective-permute-start | bytes 1572872 | tf_op jit(solution)/shard_map/ppermute | solution.py:151
  416.8 60.5 %collective-permute-start.28 = (f32[2,32,2048]{2,1,0:T(8,128)S(1)}, f32[2,32,2048]{2,1,0:T(8,128)}, u32[]{:S(2)}, u32[]{:S(2)}) collective-permute-start(f32[2,32,2048]{2,1,0:T(8,128)S(1)} %add_add_fusion.11.refs_4_.refs_1_), channel_id=1, source_target_pairs={{0,16},{8,24},{16,0},{24,8},{1,17},{9,25},{17,1},{25,9},{2,18},{10... | collective-permute-start | bytes 1572872 | tf_op jit(solution)/shard_map/ppermute | solution.py:151
  418.4 58.9 %collective-permute-start.29 = (f32[2,32,2048]{2,1,0:T(8,128)S(1)}, f32[2,32,2048]{2,1,0:T(8,128)}, u32[]{:S(2)}, u32[]{:S(2)}) collective-permute-start(f32[2,32,2048]{2,1,0:T(8,128)S(1)} %add_add_fusion.11.refs_4_.refs_1_), channel_id=1, source_target_pairs={{0,24},{8,16},{16,8},{24,0},{1,25},{9,17},{17,9},{25,1},{2,26},{10... | collective-permute-start | bytes 1572872 | tf_op jit(solution)/shard_map/ppermute | solution.py:151
  480.4 157.5 %all-gather.51.cloned.1.call-start = ((), (), s32[]{:S(2)}) async-start(), calls=%async_computation.9 | async-start | bytes 2621440 | tf_op jit(solution)/shard_map/all_gather | solution.py:129
  497.1 49.4 %collective-permute-start.32 = (f32[2,32,2048]{2,1,0:T(8,128)S(1)}, f32[2,32,2048]{2,1,0:T(8,128)}, u32[]{:S(2)}, u32[]{:S(2)}) collective-permute-start(f32[2,32,2048]{2,1,0:T(8,128)S(1)} %add_add_fusion.10.refs_4_.refs_1_), channel_id=1, source_target_pairs={{0,8},{8,0},{16,24},{24,16},{1,9},{9,1},{17,25},{25,17},{2,10},{10... | collective-permute-start | bytes 1572872 | tf_op jit(solution)/shard_map/ppermute | solution.py:151
  497.2 49.3 %collective-permute-start.33 = (f32[2,32,2048]{2,1,0:T(8,128)S(1)}, f32[2,32,2048]{2,1,0:T(8,128)}, u32[]{:S(2)}, u32[]{:S(2)}) collective-permute-start(f32[2,32,2048]{2,1,0:T(8,128)S(1)} %add_add_fusion.10.refs_4_.refs_1_), channel_id=1, source_target_pairs={{0,16},{8,24},{16,0},{24,8},{1,17},{9,25},{17,1},{25,9},{2,18},{10... | collective-permute-start | bytes 1572872 | tf_op jit(solution)/shard_map/ppermute | solution.py:151
  498.8 47.7 %collective-permute-start.34 = (f32[2,32,2048]{2,1,0:T(8,128)S(1)}, f32[2,32,2048]{2,1,0:T(8,128)}, u32[]{:S(2)}, u32[]{:S(2)}) collective-permute-start(f32[2,32,2048]{2,1,0:T(8,128)S(1)} %add_add_fusion.10.refs_4_.refs_1_), channel_id=1, source_target_pairs={{0,24},{8,16},{16,8},{24,0},{1,25},{9,17},{17,9},{25,1},{2,26},{10... | collective-permute-start | bytes 1572872 | tf_op jit(solution)/shard_map/ppermute | solution.py:151
  549.8 154.6 %all-gather.53.cloned.1.call-start = ((), (), s32[]{:S(2)}) async-start(), calls=%async_computation.10 | async-start | bytes 2621440 | tf_op jit(solution)/shard_map/all_gather | solution.py:129
  567.3 47.8 %collective-permute-start.40 = (f32[2,32,2048]{2,1,0:T(8,128)}, f32[2,32,2048]{2,1,0:T(8,128)}, u32[]{:S(2)}, u32[]{:S(2)}) collective-permute-start(f32[2,32,2048]{2,1,0:T(8,128)} %add_add_fusion.9.refs_4_.refs_1_), channel_id=1, source_target_pairs={{0,8},{8,0},{16,24},{24,16},{1,9},{9,1},{17,25},{25,17},{2,10},{10... | collective-permute-start | bytes 1572872 | tf_op jit(solution)/shard_map/ppermute | solution.py:151
  567.3 47.8 %collective-permute-start.41 = (f32[2,32,2048]{2,1,0:T(8,128)}, f32[2,32,2048]{2,1,0:T(8,128)}, u32[]{:S(2)}, u32[]{:S(2)}) collective-permute-start(f32[2,32,2048]{2,1,0:T(8,128)} %add_add_fusion.9.refs_4_.refs_1_), channel_id=1, source_target_pairs={{0,16},{8,24},{16,0},{24,8},{1,17},{9,25},{17,1},{25,9},{2,18},{10... | collective-permute-start | bytes 1572872 | tf_op jit(solution)/shard_map/ppermute | solution.py:151
  568.9 46.2 %collective-permute-start.42 = (f32[2,32,2048]{2,1,0:T(8,128)}, f32[2,32,2048]{2,1,0:T(8,128)}, u32[]{:S(2)}, u32[]{:S(2)}) collective-permute-start(f32[2,32,2048]{2,1,0:T(8,128)} %add_add_fusion.9.refs_4_.refs_1_), channel_id=1, source_target_pairs={{0,24},{8,16},{16,8},{24,0},{1,25},{9,17},{17,9},{25,1},{2,26},{10... | collective-permute-start | bytes 1572872 | tf_op jit(solution)/shard_map/ppermute | solution.py:151
  618.6 150.7 %all-gather.57.cloned.1.call-start = ((), (), s32[]{:S(2)}) async-start(), calls=%async_computation.12 | async-start | bytes 2621440 | tf_op jit(solution)/shard_map/all_gather | solution.py:129
  636.0 46.7 %collective-permute-start.49 = (f32[2,32,2048]{2,1,0:T(8,128)}, f32[2,32,2048]{2,1,0:T(8,128)}, u32[]{:S(2)}, u32[]{:S(2)}) collective-permute-start(f32[2,32,2048]{2,1,0:T(8,128)} %add_add_fusion.8.refs_4_.refs_1_), channel_id=1, source_target_pairs={{0,8},{8,0},{16,24},{24,16},{1,9},{9,1},{17,25},{25,17},{2,10},{10... | collective-permute-start | bytes 1572872 | tf_op jit(solution)/shard_map/ppermute | solution.py:151
  636.0 46.7 %collective-permute-start.50 = (f32[2,32,2048]{2,1,0:T(8,128)}, f32[2,32,2048]{2,1,0:T(8,128)}, u32[]{:S(2)}, u32[]{:S(2)}) collective-permute-start(f32[2,32,2048]{2,1,0:T(8,128)} %add_add_fusion.8.refs_4_.refs_1_), channel_id=1, source_target_pairs={{0,16},{8,24},{16,0},{24,8},{1,17},{9,25},{17,1},{25,9},{2,18},{10... | collective-permute-start | bytes 1572872 | tf_op jit(solution)/shard_map/ppermute | solution.py:151
  637.6 45.2 %collective-permute-start.51 = (f32[2,32,2048]{2,1,0:T(8,128)}, f32[2,32,2048]{2,1,0:T(8,128)}, u32[]{:S(2)}, u32[]{:S(2)}) collective-permute-start(f32[2,32,2048]{2,1,0:T(8,128)} %add_add_fusion.8.refs_4_.refs_1_), channel_id=1, source_target_pairs={{0,24},{8,16},{16,8},{24,0},{1,25},{9,17},{17,9},{25,1},{2,26},{10... | collective-permute-start | bytes 1572872 | tf_op jit(solution)/shard_map/ppermute | solution.py:151
  686.3 149.1 %all-gather.55.cloned.1.call-start = ((), (), s32[]{:S(2)}) async-start(), calls=%async_computation.11 | async-start | bytes 2621440 | tf_op jit(solution)/shard_map/all_gather | solution.py:129
  702.5 47.1 %collective-permute-start.36 = (f32[2,32,2048]{2,1,0:T(8,128)S(1)}, f32[2,32,2048]{2,1,0:T(8,128)}, u32[]{:S(2)}, u32[]{:S(2)}) collective-permute-start(f32[2,32,2048]{2,1,0:T(8,128)S(1)} %add_add_fusion.7.refs_4_.refs_1_), channel_id=1, source_target_pairs={{0,8},{8,0},{16,24},{24,16},{1,9},{9,1},{17,25},{25,17},{2,10},{10... | collective-permute-start | bytes 1572872 | tf_op jit(solution)/shard_map/ppermute | solution.py:151
  702.6 47.1 %collective-permute-start.37 = (f32[2,32,2048]{2,1,0:T(8,128)S(1)}, f32[2,32,2048]{2,1,0:T(8,128)}, u32[]{:S(2)}, u32[]{:S(2)}) collective-permute-start(f32[2,32,2048]{2,1,0:T(8,128)S(1)} %add_add_fusion.7.refs_4_.refs_1_), channel_id=1, source_target_pairs={{0,16},{8,24},{16,0},{24,8},{1,17},{9,25},{17,1},{25,9},{2,18},{10... | collective-permute-start | bytes 1572872 | tf_op jit(solution)/shard_map/ppermute | solution.py:151
  704.3 45.4 %collective-permute-start.38 = (f32[2,32,2048]{2,1,0:T(8,128)S(1)}, f32[2,32,2048]{2,1,0:T(8,128)}, u32[]{:S(2)}, u32[]{:S(2)}) collective-permute-start(f32[2,32,2048]{2,1,0:T(8,128)S(1)} %add_add_fusion.7.refs_4_.refs_1_), channel_id=1, source_target_pairs={{0,24},{8,16},{16,8},{24,0},{1,25},{9,17},{17,9},{25,1},{2,26},{10... | collective-permute-start | bytes 1572872 | tf_op jit(solution)/shard_map/ppermute | solution.py:151
  752.1 148.2 %all-gather.59.cloned.1.call-start = ((), (), s32[]{:S(2)}) async-start(), calls=%async_computation.13 | async-start | bytes 2621440 | tf_op jit(solution)/shard_map/all_gather | solution.py:129
  767.3 47.4 %collective-permute-start.45 = (f32[2,32,2048]{2,1,0:T(8,128)S(1)}, f32[2,32,2048]{2,1,0:T(8,128)}, u32[]{:S(2)}, u32[]{:S(2)}) collective-permute-start(f32[2,32,2048]{2,1,0:T(8,128)S(1)} %add_add_fusion.6.refs_4_.refs_1_), channel_id=1, source_target_pairs={{0,8},{8,0},{16,24},{24,16},{1,9},{9,1},{17,25},{25,17},{2,10},{10... | collective-permute-start | bytes 1572872 | tf_op jit(solution)/shard_map/ppermute | solution.py:151
  767.4 47.3 %collective-permute-start.46 = (f32[2,32,2048]{2,1,0:T(8,128)S(1)}, f32[2,32,2048]{2,1,0:T(8,128)}, u32[]{:S(2)}, u32[]{:S(2)}) collective-permute-start(f32[2,32,2048]{2,1,0:T(8,128)S(1)} %add_add_fusion.6.refs_4_.refs_1_), channel_id=1, source_target_pairs={{0,16},{8,24},{16,0},{24,8},{1,17},{9,25},{17,1},{25,9},{2,18},{10... | collective-permute-start | bytes 1572872 | tf_op jit(solution)/shard_map/ppermute | solution.py:151
  769.1 45.6 %collective-permute-start.47 = (f32[2,32,2048]{2,1,0:T(8,128)S(1)}, f32[2,32,2048]{2,1,0:T(8,128)}, u32[]{:S(2)}, u32[]{:S(2)}) collective-permute-start(f32[2,32,2048]{2,1,0:T(8,128)S(1)} %add_add_fusion.6.refs_4_.refs_1_), channel_id=1, source_target_pairs={{0,24},{8,16},{16,8},{24,0},{1,25},{9,17},{17,9},{25,1},{2,26},{10... | collective-permute-start | bytes 1572872 | tf_op jit(solution)/shard_map/ppermute | solution.py:151
  817.2 147.9 %all-gather.61.cloned.1.call-start = ((), (), s32[]{:S(2)}) async-start(), calls=%async_computation.14 | async-start | bytes 2621440 | tf_op jit(solution)/shard_map/all_gather | solution.py:129
  833.5 45.5 %collective-permute-start.57 = (f32[2,32,2048]{2,1,0:T(8,128)S(1)}, f32[2,32,2048]{2,1,0:T(8,128)}, u32[]{:S(2)}, u32[]{:S(2)}) collective-permute-start(f32[2,32,2048]{2,1,0:T(8,128)S(1)} %add_add_fusion.5.refs_4_.refs_1_), channel_id=1, source_target_pairs={{0,8},{8,0},{16,24},{24,16},{1,9},{9,1},{17,25},{25,17},{2,10},{10... | collective-permute-start | bytes 1572872 | tf_op jit(solution)/shard_map/ppermute | solution.py:151
  833.6 45.4 %collective-permute-start.58 = (f32[2,32,2048]{2,1,0:T(8,128)S(1)}, f32[2,32,2048]{2,1,0:T(8,128)}, u32[]{:S(2)}, u32[]{:S(2)}) collective-permute-start(f32[2,32,2048]{2,1,0:T(8,128)S(1)} %add_add_fusion.5.refs_4_.refs_1_), channel_id=1, source_target_pairs={{0,16},{8,24},{16,0},{24,8},{1,17},{9,25},{17,1},{25,9},{2,18},{10... | collective-permute-start | bytes 1572872 | tf_op jit(solution)/shard_map/ppermute | solution.py:151
  881.5 141.8 %all-gather.63.cloned.1.call-start = ((), (), s32[]{:S(2)}) async-start(), calls=%async_computation.15 | async-start | bytes 2621440 | tf_op jit(solution)/shard_map/all_gather | solution.py:129
  898.5 44.3 %collective-permute-start.65 = (f32[2,32,2048]{2,1,0:T(8,128)}, f32[2,32,2048]{2,1,0:T(8,128)}, u32[]{:S(2)}, u32[]{:S(2)}) collective-permute-start(f32[2,32,2048]{2,1,0:T(8,128)} %add_add_fusion.4.refs_4_.refs_1_), channel_id=1, source_target_pairs={{0,8},{8,0},{16,24},{24,16},{1,9},{9,1},{17,25},{25,17},{2,10},{10... | collective-permute-start | bytes 1572872 | tf_op jit(solution)/shard_map/ppermute | solution.py:151
  963.2 44.5 %collective-permute-start.62 = (f32[2,32,2048]{2,1,0:T(8,128)}, f32[2,32,2048]{2,1,0:T(8,128)}, u32[]{:S(2)}, u32[]{:S(2)}) collective-permute-start(f32[2,32,2048]{2,1,0:T(8,128)} %add_add_fusion.3.refs_4_.refs_1_), channel_id=1, source_target_pairs={{0,8},{8,0},{16,24},{24,16},{1,9},{9,1},{17,25},{25,17},{2,10},{10... | collective-permute-start | bytes 1572872 | tf_op jit(solution)/shard_map/ppermute | solution.py:151
  963.2 44.5 %collective-permute-start.63 = (f32[2,32,2048]{2,1,0:T(8,128)}, f32[2,32,2048]{2,1,0:T(8,128)}, u32[]{:S(2)}, u32[]{:S(2)}) collective-permute-start(f32[2,32,2048]{2,1,0:T(8,128)} %add_add_fusion.3.refs_4_.refs_1_), channel_id=1, source_target_pairs={{0,16},{8,24},{16,0},{24,8},{1,17},{9,25},{17,1},{25,9},{2,18},{10... | collective-permute-start | bytes 1572872 | tf_op jit(solution)/shard_map/ppermute | solution.py:151
  1021.4 50.5 %collective-permute-start.70 = (f32[2,32,2048]{2,1,0:T(8,128)}, f32[2,32,2048]{2,1,0:T(8,128)}, u32[]{:S(2)}, u32[]{:S(2)}) collective-permute-start(f32[2,32,2048]{2,1,0:T(8,128)} %add_add_fusion.2.refs_5_.refs_1_), channel_id=1, source_target_pairs={{0,8},{8,0},{16,24},{24,16},{1,9},{9,1},{17,25},{25,17},{2,10},{10... | collective-permute-start | bytes 1572872 | tf_op jit(solution)/shard_map/ppermute | solution.py:151
  1021.4 50.5 %collective-permute-start.71 = (f32[2,32,2048]{2,1,0:T(8,128)}, f32[2,32,2048]{2,1,0:T(8,128)}, u32[]{:S(2)}, u32[]{:S(2)}) collective-permute-start(f32[2,32,2048]{2,1,0:T(8,128)} %add_add_fusion.2.refs_5_.refs_1_), channel_id=1, source_target_pairs={{0,16},{8,24},{16,0},{24,8},{1,17},{9,25},{17,1},{25,9},{2,18},{10... | collective-permute-start | bytes 1572872 | tf_op jit(solution)/shard_map/ppermute | solution.py:151
  1023.1 48.8 %collective-permute-start.72 = (f32[2,32,2048]{2,1,0:T(8,128)}, f32[2,32,2048]{2,1,0:T(8,128)}, u32[]{:S(2)}, u32[]{:S(2)}) collective-permute-start(f32[2,32,2048]{2,1,0:T(8,128)} %add_add_fusion.2.refs_5_.refs_1_), channel_id=1, source_target_pairs={{0,24},{8,16},{16,8},{24,0},{1,25},{9,17},{17,9},{25,1},{2,26},{10... | collective-permute-start | bytes 1572872 | tf_op jit(solution)/shard_map/ppermute | solution.py:151
  1025.1 55.9 %collective-permute-start.69 = (f32[2,2,32,2048]{3,2,1,0:T(8,128)S(1)}, f32[2,2,32,2048]{3,2,1,0:T(8,128)S(1)}, u32[]{:S(2)}, u32[]{:S(2)}) collective-permute-start(f32[2,2,32,2048]{3,2,1,0:T(8,128)S(1)} %get-tuple-element.85.refs_4_), channel_id=1, source_target_pairs={{0,4},{4,0},{1,5},{5,1},{2,6},{6,2},{3,7},{7,3},{8,12},{12,8},{9,1... | collective-permute-start | bytes 3145736 | tf_op jit(solution)/shard_map/ppermute | solution.py:136
  (128 other events, 2561.8 us)
Sparse Core Ops, SparseCore 0:
  10.2 48.3 all-gather.32
  60.2 44.4 all-gather.34
  106.2 44.4 all-gather.36
  152.2 44.4 all-gather.40
  198.1 44.4 all-gather.38
  261.9 43.6 all-gather.42
  331.4 43.6 all-gather.44
  400.4 43.7 all-gather.46
  480.6 43.7 all-gather.48
  550.0 43.7 all-gather.50
  618.7 43.7 all-gather.52
  686.4 43.7 all-gather.56
  752.2 43.8 all-gather.54
  817.3 43.9 all-gather.58
  881.6 44.0 all-gather.60
  946.4 44.1 all-gather.62
